TPU v7x, 128 devices: a whole 4x4x4 slice. The times are simulated.
128 devices in a mesh: req: 32 (over z, x, core), tp: 4 (over y).
Axes of the slice: x: 4, y: 4, z: 4, core: 2. Of those that a mesh axis runs over, the one named last changes fastest.
Arguments:
- tokens: bfloat16 [12288, 5120], P('req'), may hold values from -40 to 40
- w_query: bfloat16 [5120, 2560], P(None, 'tp'), may hold values from -0.125 to 0.125
- query_bias: float32 [2560], P('tp'), may hold values from -24 to 24
- w_keyval: bfloat16 [5120, 1024], P(None, 'tp'), may hold values from -0.21875 to 0.21875
- keyval_bias: float32 [1024], P('tp'), may hold values from -2.5 to 2.5
- w_out: bfloat16 [2560, 5120], P('tp'), may hold values from -0.25 to 0.25
- attn_gain: float32 [5120], replicated, may hold values from 0.25 to 1.75
- final_norm_gain: float32 [5120], replicated, may hold values from 0.25 to 1.75
- head_weight: bfloat16 [5120, 76032], P(None, ('req', 'tp')), may hold values from -0.25 to 0.25
- kv_pool: bfloat16 [851968, 4, 256], P('req', 'tp'), may hold values from -17 to 17
- cache_len: int32 [512], replicated, may hold values from 256 to 3072, as said below
Outputs:
- states: bfloat16 [12288, 5120], P('req', 'tp')
- new_kv: bfloat16 [12288, 4, 256], P('req', 'tp')
- row_norms: float32 [512], P('req')
- logit_max: float32 [512], replicated
- logits: float32 [512, 76032], P(None, ('req', 'tp'))
Inputs may be any that keep to these rules, and one draw needn't show every extreme that they name: `cache_len`: every cache holds 256 or 3072 rows. Exactly 64 requests hold 3072; requests i * 16 to i * 16 + 15 hold at most 8 of them for every i, and exactly 8 for some i, so their caches fill at most 26624 rows, and exactly 26624 for some i.
All inputs are finite; a program needn't handle non-finite values.
Results may differ from a plain program's by a relative error of at most 0.014.
Values may be sent and summed in bfloat16 or wider, within the bound.
A program may use at most 192 MiB of HBM per device.

v0:
```python
import math

import jax
import jax.numpy as jnp
from jax import lax
from jax.sharding import PartitionSpec as P

HD = 128
GROUP = 5
NEW = 24
LONG = 3072


THETA = 1000000.0
EPS = 1e-06
NEG = -1e30


def rope_rotate(vectors, positions):
    head_width = vectors.shape[-1]
    halfway = head_width // 2
    frequency = THETA ** (-(jnp.arange(halfway, dtype=jnp.float32) * (2.0 / head_width)))
    angles = positions[..., None] * frequency
    cosine = jnp.cos(angles)
    sine_part = jnp.sin(angles)
    front_part = vectors[..., :halfway]
    back_part = vectors[..., halfway:]
    return jnp.concatenate(
        [front_part * cosine - back_part * sine_part, back_part * cosine + front_part * sine_part],
        axis=-1,
    )


def online_update(state_in, scores, value_matrix):
    running_max, totals, weighted = state_in
    new_max = jnp.maximum(running_max, jnp.max(scores, axis=-1))
    rescale = jnp.exp(running_max - new_max)
    weight_matrix = jnp.exp(scores - new_max[..., None])
    totals = totals * rescale + jnp.sum(weight_matrix, axis=-1)
    weighted = weighted * rescale[..., None] + jnp.einsum(
        "amz,zav->amv",
        weight_matrix.astype(jnp.bfloat16),
        value_matrix,
        preferred_element_type=jnp.float32,
    )
    return (new_max, totals, weighted)


def attend_windows(query_rows, pool_part, leading_row, req_starts, req_lens, start_state):
    head_width = query_rows.shape[-1]
    kv_local = query_rows.shape[0]
    query_count = query_rows.shape[1]
    req_count = req_starts.shape[0]
    row_span = query_count // req_count
    part_rows = pool_part.shape[0]
    window_rows = min(LONG, part_rows)
    batch_size = math.gcd(req_count, 4)
    batch_count = req_count // batch_size

    def per_request(query_block, begin, length, state_max, state_totals, state_weighted):
        first = jnp.clip(begin - leading_row, 0, part_rows - window_rows)
        window = lax.dynamic_slice_in_dim(pool_part, first, window_rows, 0)
        row_index = leading_row + first + jnp.arange(window_rows, dtype=jnp.int32)
        inside = (row_index >= begin) & (row_index < begin + length)
        scores = jnp.einsum(
            "mjl,wml->mjw",
            query_block,
            window[..., :head_width],
            preferred_element_type=jnp.float32,
        )
        scores = jnp.where(inside[None, None, :], scores, -jnp.inf)
        return online_update(
            (state_max, state_totals, state_weighted), scores, window[..., head_width:]
        )

    def split_requests(array_in):
        moved = jnp.moveaxis(
            array_in.reshape((kv_local, req_count, row_span) + array_in.shape[2:]), 1, 0
        )
        return moved.reshape((batch_count, batch_size) + moved.shape[1:])

    def join_requests(array_in):
        merged = array_in.reshape((req_count,) + array_in.shape[2:])
        return jnp.moveaxis(merged, 0, 1).reshape((kv_local, query_count) + merged.shape[3:])

    def one_batch(inputs):
        return jax.vmap(per_request)(*inputs)

    batched = (
        split_requests(query_rows),
        req_starts.reshape(batch_count, batch_size),
        req_lens.reshape(batch_count, batch_size),
        split_requests(start_state[0]),
        split_requests(start_state[1]),
        split_requests(start_state[2]),
    )
    result = lax.map(one_batch, batched)
    return tuple((join_requests(part_state) for part_state in result))


def local(
    tokens,
    w_query,
    query_bias,
    w_keyval,
    keyval_bias,
    w_out,
    attn_gain,
    final_norm_gain,
    head_weight,
    kv_pool,
    cache_len,
):
    groups = lax.axis_size("req")
    my_group = lax.axis_index("req")
    tp_count = lax.axis_size("tp")
    tp_index = lax.axis_index("tp")
    tok_rows = tokens.shape[0]
    model_width = tokens.shape[1]
    per_group = tok_rows // NEW
    kv_local = kv_pool.shape[1]
    lens_grid = cache_len.reshape(groups, per_group)
    my_lens = lax.dynamic_slice_in_dim(lens_grid, my_group, 1, 0)[0]
    my_starts = jnp.cumsum(my_lens) - my_lens
    source = tokens.astype(jnp.float32)
    mean_square = jnp.mean(source * source, axis=1, keepdims=True)
    normed = (source / jnp.sqrt(mean_square + EPS) * attn_gain[None, :]).astype(jnp.bfloat16)
    query_raw = jnp.dot(normed, w_query, preferred_element_type=jnp.float32) + query_bias[None, :]
    keyval_raw = (
        jnp.dot(normed, w_keyval, preferred_element_type=jnp.float32) + keyval_bias[None, :]
    )
    positions = (my_lens[:, None] + jnp.arange(NEW, dtype=jnp.int32)[None, :]).astype(jnp.float32)
    query_heads = query_raw.reshape(per_group, NEW, kv_local, GROUP, HD)
    queries = (
        rope_rotate(query_heads, positions[:, :, None, None]) * (1.0 / math.sqrt(HD))
    ).astype(jnp.bfloat16)
    keyval_heads = keyval_raw.reshape(per_group, NEW, kv_local, 2, HD)
    key_new = rope_rotate(keyval_heads[:, :, :, 0, :], positions[:, :, None]).astype(jnp.bfloat16)
    value_new = keyval_heads[:, :, :, 1, :].astype(jnp.bfloat16)
    new_kv = jnp.concatenate([key_new, value_new], axis=-1).reshape(tok_rows, kv_local, 2 * HD)
    row_span = NEW * GROUP
    query_count = per_group * row_span
    query_rows = jnp.transpose(queries, (2, 0, 1, 3, 4)).reshape(kv_local, query_count, HD)
    start_state = (
        jnp.full((kv_local, query_count), NEG, jnp.float32),
        jnp.zeros((kv_local, query_count), jnp.float32),
        jnp.zeros((kv_local, query_count, HD), jnp.float32),
    )
    carry_state = attend_windows(query_rows, kv_pool, 0, my_starts, my_lens, start_state)
    key_rows = key_new.reshape(tok_rows, kv_local, HD)
    value_rows = value_new.reshape(tok_rows, kv_local, HD)
    new_scores = jnp.einsum(
        "kqd,mkd->kqm", query_rows, key_rows, preferred_element_type=jnp.float32
    )
    query_token = jnp.arange(query_count, dtype=jnp.int32) // GROUP
    key_token = jnp.arange(tok_rows, dtype=jnp.int32)
    allowed = (query_token[:, None] // NEW == key_token[None, :] // NEW) & (
        key_token[None, :] <= query_token[:, None]
    )
    new_scores = jnp.where(allowed[None], new_scores, -jnp.inf)
    carry_state = online_update(carry_state, new_scores, value_rows)
    attention = (carry_state[2] / carry_state[1][..., None]).astype(jnp.bfloat16)
    attention = jnp.transpose(
        attention.reshape(kv_local, per_group, NEW, GROUP, HD), (1, 2, 0, 3, 4)
    ).reshape(tok_rows, kv_local * GROUP * HD)
    partial_value = jnp.dot(attention, w_out, preferred_element_type=jnp.float32)
    width_local = model_width // tp_count
    summed = lax.psum(partial_value.astype(jnp.bfloat16), "tp").astype(jnp.float32)
    states_full = (source + summed).astype(jnp.bfloat16)
    states = lax.dynamic_slice_in_dim(states_full, tp_index * width_local, width_local, 1)
    last_rows = states_full.reshape(per_group, NEW, model_width)[:, NEW - 1, :].astype(jnp.float32)
    row_norms = jnp.sqrt(jnp.mean(last_rows * last_rows, axis=1) + EPS)
    final_rows = (last_rows / row_norms[:, None] * final_norm_gain[None, :]).astype(jnp.bfloat16)
    logits = jnp.dot(
        lax.all_gather(final_rows, "req", axis=0, tiled=True),
        head_weight,
        preferred_element_type=jnp.float32,
    )
    logit_max = lax.pmax(jnp.max(logits, axis=1), ("req", "tp"))
    return (states, new_kv, row_norms, logit_max, logits)


def solution(mesh):
    return jax.shard_map(
        local,
        mesh=mesh,
        in_specs=(
            P("req", None),
            P(None, "tp"),
            P("tp"),
            P(None, "tp"),
            P("tp"),
            P("tp", None),
            P(),
            P(),
            P(None, ("req", "tp")),
            P("req", "tp", None),
            P(),
        ),
        out_specs=(P("req", "tp"), P("req", "tp", None), P("req"), P(), P(None, ("req", "tp"))),
        check_vma=False,
    )
```

profile of v0, /device:TPU:0, one launch (start us, length us, event | category | flops | bytes accessed | tf_op | source)
XLA Modules:
  0.0 364.4 jit_solution(11805179985593253152)
XLA Ops:
  7.3 3.1 fusion.27
  10.7 3.6 fusion.29
  16.1 4.2 %convolution_add_fusion.1 = f32[384,640]{1,0:T(8,128)} fusion(bf16[384,5120]{1,0:T(8,128)(2,1)S(1)} %fusion.29, bf16[5120,640]{1,0:T(8,128)(2,1)S(1)} %copy-done.12, f32[640]{0:T(1024)S(1)} %copy-done.13), kind=kOutput, calls=%fused_computation.58 | convolution fusion | flops 2516828160 | bytes 11471360 | tf_op jit(solution)/shard_map/dot_general | solution.py:128
  23.5 4.2 %multiply_subtract_fusion = (f32[16,24,1,5,64]{4,3,1,0,2:T(8,128)}, f32[16,24,1,5,64]{4,3,1,0,2:T(8,128)}) fusion(f32[16,24,1,5,128]{4,3,1,0,2:T(8,128)} %reshape.555, f32[16,24,64]{2,1,0:T(8,128)S(1)} %get-tuple-element.120, f32[16,24,64]{2,1,0:T(8,128)S(1)} %get-tuple-element.119), kind=kLoop, calls=%fused_computation.56 | loop fusion | flops 737280 | bytes 2162688 | tf_op jit(solution)/shard_map/sub | solution.py:29
  38.9 3.3 convolution_add_fusion.2
  45.7 81.0 %while.17 = (s32[]{:T(128)}, f32[4,4,1,120]{3,1,2,0:T(4,128)S(1)}, f32[4,4,1,120]{3,1,2,0:T(4,128)S(1)}, f32[4,4,1,120,128]{4,3,1,2,0:T(8,128)}, s32[4,4]{1,0:T(...) while((s32[]{:T(128)}, f32[4,4,1,120]{3,1,2,0:T(4,128)S(1)}, ...), condition=%wide.region_5.6_spmd, body=%wide.region_2.5_spmd.sunk | while | flops 766884224 | bytes 52985684 | solution.py:97
  46.1 12.2 %while.18 = (s32[]{:T(128)}, bf16[26624,1,256]{2,0,1:T(8,128)(2,1)}, s32[4,3]{1,0:T(4,128)S(1)}, bf16[4,3072,1,256]{3,1,2,0:T(8,128)(2,1)}, s32[]{:T(128)}) while((s32[]{:T(128)}, bf16[26624,1,256]{2,0,1:T(8,128)(2,1)}, s32[4,3]{1,0:T(4,128)S(1)}, bf16[4,3072,1,256]{3,1,2,0:T(8,128)(2,1)}, s32[]{:T(128)}) %tuple.62), condition=%wide.while_cond, body=%wide.while_body.sunk | while | flops 2 | bytes 3145833 | solution.py:62
  46.1 3.2 bitcast_dynamic-update-slice_fusion.3
  49.3 3.0 bitcast_dynamic-update-slice_fusion.3
  52.3 3.0 bitcast_dynamic-update-slice_fusion.3
  55.3 3.0 bitcast_dynamic-update-slice_fusion.3
  58.3 4.2 %select_reduce_fusion.2 = (f32[4,120]{1,0:T(4,128)S(1)}, f32[4,120,3072]{2,1,0:T(8,128)S(1)}) fusion(pred[4,3072]{1,0:T(4,128)(4,1)S(1)} %fusion.90, bf16[4,3072,1,256]{3,1,0,2:T(8,128)(2,1)} %bitcast.118, bf16[1,4,1,120,128]{4,1,0,3,2:T(4,128)(2,1)S(1)} %constant_dynamic-slice_fusion.8), kind=kOutput, calls=%fused_computation.3.clone.1 | convolution fusion | flops 380436000 | bytes 9181056 | tf_op jit(solution)/shard_map/while/body/eval_jaxpr/vmap(mjl,wml->mjw)/dot_general | solution.py:65
  66.4 12.1 %while.18 = (s32[]{:T(128)}, bf16[26624,1,256]{2,0,1:T(8,128)(2,1)}, s32[4,3]{1,0:T(4,128)S(1)}, bf16[4,3072,1,256]{3,1,2,0:T(8,128)(2,1)}, s32[]{:T(128)}) while((s32[]{:T(128)}, bf16[26624,1,256]{2,0,1:T(8,128)(2,1)}, s32[4,3]{1,0:T(4,128)S(1)}, bf16[4,3072,1,256]{3,1,2,0:T(8,128)(2,1)}, s32[]{:T(128)}) %tuple.62), condition=%wide.while_cond, body=%wide.while_body.sunk | while | flops 2 | bytes 3145833 | solution.py:62
  66.4 3.0 bitcast_dynamic-update-slice_fusion.3
  69.4 3.0 bitcast_dynamic-update-slice_fusion.3
  75.4 3.0 bitcast_dynamic-update-slice_fusion.3
  78.4 4.2 %select_reduce_fusion.2 = (f32[4,120]{1,0:T(4,128)S(1)}, f32[4,120,3072]{2,1,0:T(8,128)S(1)}) fusion(pred[4,3072]{1,0:T(4,128)(4,1)S(1)} %fusion.90, bf16[4,3072,1,256]{3,1,0,2:T(8,128)(2,1)} %bitcast.118, bf16[1,4,1,120,128]{4,1,0,3,2:T(4,128)(2,1)S(1)} %constant_dynamic-slice_fusion.8), kind=kOutput, calls=%fused_computation.3.clone.1 | convolution fusion | flops 380436000 | bytes 9181056 | tf_op jit(solution)/shard_map/while/body/eval_jaxpr/vmap(mjl,wml->mjw)/dot_general | solution.py:65
  86.5 12.1 %while.18 = (s32[]{:T(128)}, bf16[26624,1,256]{2,0,1:T(8,128)(2,1)}, s32[4,3]{1,0:T(4,128)S(1)}, bf16[4,3072,1,256]{3,1,2,0:T(8,128)(2,1)}, s32[]{:T(128)}) while((s32[]{:T(128)}, bf16[26624,1,256]{2,0,1:T(8,128)(2,1)}, s32[4,3]{1,0:T(4,128)S(1)}, bf16[4,3072,1,256]{3,1,2,0:T(8,128)(2,1)}, s32[]{:T(128)}) %tuple.62), condition=%wide.while_cond, body=%wide.while_body.sunk | while | flops 2 | bytes 3145833 | solution.py:62
  86.5 3.0 bitcast_dynamic-update-slice_fusion.3
  95.6 3.0 bitcast_dynamic-update-slice_fusion.3
  98.6 4.2 %select_reduce_fusion.2 = (f32[4,120]{1,0:T(4,128)S(1)}, f32[4,120,3072]{2,1,0:T(8,128)S(1)}) fusion(pred[4,3072]{1,0:T(4,128)(4,1)S(1)} %fusion.90, bf16[4,3072,1,256]{3,1,0,2:T(8,128)(2,1)} %bitcast.118, bf16[1,4,1,120,128]{4,1,0,3,2:T(4,128)(2,1)S(1)} %constant_dynamic-slice_fusion.8), kind=kOutput, calls=%fused_computation.3.clone.1 | convolution fusion | flops 380436000 | bytes 9181056 | tf_op jit(solution)/shard_map/while/body/eval_jaxpr/vmap(mjl,wml->mjw)/dot_general | solution.py:65
  106.7 12.1 %while.18 = (s32[]{:T(128)}, bf16[26624,1,256]{2,0,1:T(8,128)(2,1)}, s32[4,3]{1,0:T(4,128)S(1)}, bf16[4,3072,1,256]{3,1,2,0:T(8,128)(2,1)}, s32[]{:T(128)}) while((s32[]{:T(128)}, bf16[26624,1,256]{2,0,1:T(8,128)(2,1)}, s32[4,3]{1,0:T(4,128)S(1)}, bf16[4,3072,1,256]{3,1,2,0:T(8,128)(2,1)}, s32[]{:T(128)}) %tuple.62), condition=%wide.while_cond, body=%wide.while_body.sunk | while | flops 2 | bytes 3145833 | solution.py:62
  106.7 3.0 bitcast_dynamic-update-slice_fusion.3
  109.7 3.0 bitcast_dynamic-update-slice_fusion.3
  115.7 3.0 bitcast_dynamic-update-slice_fusion.3
  118.7 4.2 %select_reduce_fusion.2 = (f32[4,120]{1,0:T(4,128)S(1)}, f32[4,120,3072]{2,1,0:T(8,128)S(1)}) fusion(pred[4,3072]{1,0:T(4,128)(4,1)S(1)} %fusion.90, bf16[4,3072,1,256]{3,1,0,2:T(8,128)(2,1)} %bitcast.118, bf16[1,4,1,120,128]{4,1,0,3,2:T(4,128)(2,1)S(1)} %constant_dynamic-slice_fusion.8), kind=kOutput, calls=%fused_computation.3.clone.1 | convolution fusion | flops 380436000 | bytes 9181056 | tf_op jit(solution)/shard_map/while/body/eval_jaxpr/vmap(mjl,wml->mjw)/dot_general | solution.py:65
  129.9 7.6 %convolution_convert_fusion = bf16[384,5120]{1,0:T(8,128)(2,1)} fusion(bf16[384,640]{1,0:T(8,128)(2,1)S(1)} %reshape_transpose_reshape.16, bf16[640,5120]{1,0:T(8,128)(2,1)} %param.18), kind=kOutput, calls=%fused_computation.45 | convolution fusion | flops 2518548480 | bytes 10977280 | tf_op jit(solution)/shard_map/dot_general | solution.py:166
  137.5 91.1 %all-reduce.3.cloned.1.call-done = bf16[384,5120]{1,0:T(8,128)(2,1)} async-done(((bf16[384,5120]{1,0:T(8,128)(2,1)}), bf16[384,5120]{1,0:T(8,128)(2,1)}) %all-reduce.3.cloned.1.call-update) | async-done | bytes 3932176 | tf_op jit(solution)/shard_map/psum | solution.py:168
  228.6 4.8 %fusion.30 = bf16[384,5120]{1,0:T(8,128)(2,1)S(1)} fusion(bf16[384,5120]{1,0:T(8,128)(2,1)} %param.13, bf16[384,5120]{1,0:T(8,128)(2,1)} %all-reduce.3.cloned.1.call-done), kind=kLoop, calls=%fused_computation.44 | loop fusion | flops 7864320 | bytes 11796480 | tf_op jit(solution)/shard_map/convert_element_type | solution.py:169
  239.7 44.5 %all-gather.2.cloned.1.call-done = bf16[512,5120]{1,0:T(8,128)(2,1)} async-done(((bf16[16,5120]{1,0:T(8,128)(2,1)}), bf16[512,5120]{1,0:T(8,128)(2,1)}) %all-gather.2.cloned.1.call-update) | async-done | bytes 5242896 | tf_op jit(solution)/shard_map/all_gather | solution.py:175
  284.2 8.8 %fusion.72 = (f32[512]{0:T(512)S(1)}, f32[512,594]{0,1:T(8,128)}) fusion(bf16[512,5120]{1,0:T(8,128)(2,1)} %all-gather.2.cloned.1.call-done, bf16[5120,594]{0,1:T(8,128)(2,1)} %param.21), kind=kOutput, calls=%fused_computation.122 | convolution fusion | flops 3114574336 | bytes 12544000 | tf_op jit(solution)/shard_map/dot_general | solution.py:174
  293.0 64.5 %pmax.7 = f32[512]{0:T(512)} all-reduce(f32[512]{0:T(512)S(1)} %get-tuple-element.123), channel_id=1, replica_groups=mesh['req'=32,'tp'=4] {'req','tp'}, use_global_device_ids=true, to_apply=%region_11.12 | all-reduce | flops 512 | bytes 4096 | tf_op jit(solution)/shard_map/pmax | solution.py:179
  (150 shorter events, 56.6 us)
Async XLA Ops:
  7.2 31.7 %copy-start = (bf16[5120,256]{1,0:T(8,128)(2,1)S(1)}, bf16[5120,256]{1,0:T(8,128)(2,1)}, u32[]{:S(2)}) copy-start(bf16[5120,256]{1,0:T(8,128)(2,1)} %param.16) | copy-start | bytes 7864324
  7.2 3.3 copy-start.10
  7.2 3.5 copy-start.8
  7.2 221.4 %all-reduce.3.cloned.1.call-start = ((), (), s32[]{:S(2)}) async-start(), calls=%async_computation | async-start | bytes 7864320 | tf_op jit(solution)/shard_map/psum | solution.py:168
  10.6 5.5 %copy-start.12 = (bf16[5120,640]{1,0:T(8,128)(2,1)S(1)}, bf16[5120,640]{1,0:T(8,128)(2,1)}, u32[]{:S(2)}) copy-start(bf16[5120,640]{1,0:T(8,128)(2,1)} %param.14) | copy-start | bytes 19660804
  10.7 5.5 %copy-start.13 = (f32[640]{0:T(1024)S(1)}, f32[640]{0:T(1024)}, u32[]{:S(2)}) copy-start(f32[640]{0:T(1024)} %param.15) | copy-start | bytes 7684
  14.2 1.9 copy-start.4
  30.1 8.8 %copy-start.14 = (f32[256]{0:T(256)S(1)}, f32[256]{0:T(256)}, u32[]{:S(2)}) copy-start(f32[256]{0:T(256)} %param.17) | copy-start | bytes 3076
  45.7 81.2 %copy-start.5 = (f32[1920,64]{1,0:T(8,128)S(1)}, f32[1920,64]{1,0:T(8,128)}, u32[]{:S(2)}) copy-start(f32[1920,64]{1,0:T(8,128)} %concatenate.59) | copy-start | bytes 1474564
  45.7 81.2 %copy-start.6 = (f32[1920,64]{1,0:T(8,128)S(1)}, f32[1920,64]{1,0:T(8,128)}, u32[]{:S(2)}) copy-start(f32[1920,64]{1,0:T(8,128)} %concatenate.60) | copy-start | bytes 1474564
  58.3 4.3 %copy-start.2 = (bf16[4,3072,1,256]{3,1,2,0:T(8,128)(2,1)S(1)}, bf16[4,3072,1,256]{3,1,2,0:T(8,128)(2,1)}, u32[]{:S(2)}) copy-start(bf16[4,3072,1,256]{3,1,2,0:T(8,128)(2,1)} %get-tuple-element.216) | copy-start | bytes 18874372 | tf_op jit(solution)/shard_map/while
  78.4 4.2 %copy-start.2 = (bf16[4,3072,1,256]{3,1,2,0:T(8,128)(2,1)S(1)}, bf16[4,3072,1,256]{3,1,2,0:T(8,128)(2,1)}, u32[]{:S(2)}) copy-start(bf16[4,3072,1,256]{3,1,2,0:T(8,128)(2,1)} %get-tuple-element.216) | copy-start | bytes 18874372 | tf_op jit(solution)/shard_map/while
  98.6 4.2 %copy-start.2 = (bf16[4,3072,1,256]{3,1,2,0:T(8,128)(2,1)S(1)}, bf16[4,3072,1,256]{3,1,2,0:T(8,128)(2,1)}, u32[]{:S(2)}) copy-start(bf16[4,3072,1,256]{3,1,2,0:T(8,128)(2,1)} %get-tuple-element.216) | copy-start | bytes 18874372 | tf_op jit(solution)/shard_map/while
  118.7 4.2 %copy-start.2 = (bf16[4,3072,1,256]{3,1,2,0:T(8,128)(2,1)S(1)}, bf16[4,3072,1,256]{3,1,2,0:T(8,128)(2,1)}, u32[]{:S(2)}) copy-start(bf16[4,3072,1,256]{3,1,2,0:T(8,128)(2,1)} %get-tuple-element.216) | copy-start | bytes 18874372 | tf_op jit(solution)/shard_map/while
  126.9 1.5 copy-start.7
  137.5 98.3 %copy-start.9 = (f32[5120]{0:T(1024)S(1)}, f32[5120]{0:T(1024)}, u32[]{:S(2)}) copy-start(f32[5120]{0:T(1024)} %param.20) | copy-start | bytes 61444
  137.5 146.7 %all-gather.2.cloned.1.call-start = ((), (), s32[]{:S(2)}) async-start(), calls=%async_computation.1 | async-start | bytes 5406720 | tf_op jit(solution)/shard_map/all_gather | solution.py:175
  233.4 1.9 copy-start.3
  235.8 57.2 %copy-start.11 = (f32[16]{0:T(128)}, f32[16]{0:T(128)S(1)}, u32[]{:S(2)}) copy-start(f32[16]{0:T(128)S(1)} %add_sqrt_fusion.1) | copy-start | bytes 196
  284.2 73.4 %copy-start.1 = (bf16[5120,256]{1,0:T(8,128)(2,1)S(1)}, bf16[5120,256]{1,0:T(8,128)(2,1)}, u32[]{:S(2)}) copy-start(bf16[5120,256]{1,0:T(8,128)(2,1)} %param.16) | copy-start | bytes 7864324
Sparse Core Ops, SparseCore 0:
  137.6 90.9 all-reduce.2
  236.8 47.3 all-gather.1
where the time goes:
time: 366 us; the launch traced here: 364 us
  waiting for transfers between devices  136 us (37%)
  local copies, waits for them, and re-layouts  69.7 us (19%)
  blocking collectives  64.5 us (18%)
  matrix products  51.4 us (14%)
  other arithmetic  28.1 us (8%)
  between operations  14.4 us (4%)
    psum x1, waiting for transfers between devices, local(): lax.psum(partial_value.astype(jnp.bfloat16), 'tp').astype(jnp.float32)  91.1 us
    pmax x1, blocking collectives, local(): logit_max = lax.pmax(jnp.max(logits, axis=1), ('req', 'tp'))  64.5 us
    gather x32, local copies, waits for them, and re-layouts  48.3 us
    all_gather x1, waiting for transfers between devices, local(): lax.all_gather(final_rows, 'req', axis=0, tiled=True)  44.5 us
    dot_general x4, matrix products, per_request(): jnp.einsum('mjl,wml->mjw', query_block, window[..., :head_width], preferr...  16.9 us
    dot_general x5, matrix products, online_update(): jnp.einsum('amz,zav->amv', weight_matrix.astype(jnp.bfloat16), value_matr...  9.56 us
    dot_general x1, matrix products, local(): jnp.dot(lax.all_gather(final_rows, 'req', axis=0, tiled=True), head_weigh...  8.84 us
    dot_general x1, matrix products, local(): jnp.dot(attention, w_out, preferred_element_type=jnp.float32)  7.58 us
  transfers between devices with their start and end apart: 2, of which 2 were waited for; matrix products, arithmetic and copies ran while one was open for 1% of the time, Pallas kernels for 0%

commit v1 on v0

v1 whole, which is shorter than its diff:
```python
import math

import jax
import jax.numpy as jnp
import numpy as np
from jax import lax
from jax.experimental import pallas as pl
from jax.experimental.pallas import tpu as pltpu
from jax.sharding import PartitionSpec as P

D = 5120
HD = 128
GROUP = 5
NEW = 24
SHORT = 256
LONG = 3072
REQ_DEV = 16
POOL = 26624
ROWS = REQ_DEV * NEW
QW = GROUP * HD
KW = 2 * HD
THETA = 1000000.0
EPS = 1e-06
NEG = -1e30

KC = 1024
NKC = D // KC
PC = 2048
NPC = POOL // PC
QR = 128


def rope_tables():
    freq = np.float32(THETA) ** (-(np.arange(HD // 2, dtype=np.float32) * np.float32(2.0 / HD)))
    pos = np.concatenate([SHORT + np.arange(NEW), LONG + np.arange(NEW)]).astype(np.float32)
    ang = (pos[:, None] * freq[None, :].astype(np.float32)).astype(np.float64)
    cos = np.cos(ang).astype(np.float32)
    sin = np.sin(ang).astype(np.float32)
    return np.concatenate([cos, cos, -sin, sin], axis=1)


def attn_kernel(
    lens_ref,
    tok_hbm,
    wq_hbm,
    wkv_hbm,
    qb_ref,
    kvb_ref,
    gain_ref,
    cs_ref,
    pool_hbm,
    newkv_ref,
    attn_ref,
    last_ref,
    tok_v,
    w_v,
    pool_v,
    acc,
    ss,
    tok_sem,
    wq_sem,
    wkv_sem,
    pool_sem,
):
    def tok_copy(k):
        c = pl.ds(pl.multiple_of(k * KC, KC), KC)
        return pltpu.make_async_copy(tok_hbm.at[:, c], tok_v.at[:, c], tok_sem.at[k])

    def wq_copy(k):
        c = pl.ds(pl.multiple_of(k * KC, KC), KC)
        return pltpu.make_async_copy(wq_hbm.at[c, :], w_v.at[c, pl.ds(0, QW)], wq_sem.at[k])

    def wkv_copy(k):
        c = pl.ds(pl.multiple_of(k * KC, KC), KC)
        return pltpu.make_async_copy(wkv_hbm.at[c, :], w_v.at[c, pl.ds(QW, KW)], wkv_sem.at[k])

    def pool_copy(k):
        c = pl.ds(pl.multiple_of(k * PC, PC), PC)
        return pltpu.make_async_copy(pool_hbm.at[c, :], pool_v.at[c, :], pool_sem.at[k])

    for k in range(NKC):
        tok_copy(k).start()
        wq_copy(k).start()
        wkv_copy(k).start()
    for k in range(NPC):
        pool_copy(k).start()

    ss[...] = jnp.zeros_like(ss)
    acc[...] = jnp.zeros_like(acc)

    @pl.loop(0, NKC)
    def _(k):
        tok_copy(k).wait()
        wq_copy(k).wait()
        wkv_copy(k).wait()
        c = pl.ds(pl.multiple_of(k * KC, KC), KC)
        x = tok_v[:, c].astype(jnp.float32)
        sq = x * x
        part = sq[:, 0:HD]
        for i in range(1, KC // HD):
            part = part + sq[:, i * HD : (i + 1) * HD]
        ss[...] += part
        xg = (x * gain_ref[:, c]).astype(jnp.bfloat16)
        acc[...] += jnp.dot(xg, w_v[c, :], preferred_element_type=jnp.float32)

    rstd = 1.0 / jnp.sqrt(jnp.sum(ss[...], axis=1, keepdims=True) * (1.0 / D) + EPS)
    ss[...] = jnp.broadcast_to(rstd, ss.shape)

    row = lax.broadcasted_iota(jnp.int32, (QR, HD), 0)
    col = lax.broadcasted_iota(jnp.int32, (QR, HD), 1)
    token = row
    for g in range(1, GROUP + 1):
        token = token - jnp.where(row >= g * NEW, NEW, 0)
    causal = (col <= token) & (col < NEW)
    base = lax.axis_index("req") * REQ_DEV
    scale = 1.0 / math.sqrt(HD)

    def request(r, carry):
        begin, waited = carry
        length = lens_ref[base + r]
        is_long = length > SHORT
        need = (begin + length + (PC - 1)) // PC

        def wait_one(i, c):
            pool_copy(i).wait()
            return c

        lax.fori_loop(waited, need, wait_one, 0)
        rows = pl.ds(pl.multiple_of(r * NEW, 8), NEW)
        table = pl.ds(pl.multiple_of(jnp.where(is_long, NEW, 0), 8), NEW)
        cos = cs_ref[table, pl.ds(0, HD)]
        sin = cs_ref[table, pl.ds(HD, HD)]
        rs = ss[rows, :]

        def rope(v):
            return v * cos + pltpu.roll(v, HD // 2, 1) * sin

        heads = []
        for g in range(GROUP):
            c = slice(g * HD, (g + 1) * HD)
            heads.append(rope(acc[rows, c] * rs + qb_ref[:, c]) * scale)
        heads.append(jnp.zeros((QR - GROUP * NEW, HD), jnp.float32))
        q = jnp.concatenate(heads, axis=0).astype(jnp.bfloat16)
        key = rope(acc[rows, QW : QW + HD] * rs + kvb_ref[:, 0:HD])
        value = acc[rows, QW + HD : QW + KW] * rs + kvb_ref[:, HD:KW]
        acc[rows, QW : QW + HD] = key
        acc[rows, QW + HD : QW + KW] = value
        fill = jnp.zeros((HD - NEW, HD), jnp.float32)
        key = jnp.concatenate([key, fill], axis=0).astype(jnp.bfloat16)
        value = jnp.concatenate([value, fill], axis=0).astype(jnp.bfloat16)

        def scores_of(k):
            return lax.dot_general(q, k, (((1,), (1,)), ((), ())), preferred_element_type=jnp.float32)

        def finish(n_chunks, width):
            s_new = jnp.where(causal, scores_of(key), NEG)
            chunks = []
            m = jnp.max(s_new, axis=1, keepdims=True)
            for i in range(n_chunks):
                w = pl.ds(pl.multiple_of(begin + i * width, SHORT), width)
                s = scores_of(pool_v[w, pl.ds(0, HD)])
                chunks.append((s, w))
                m = jnp.maximum(m, jnp.max(s, axis=1, keepdims=True))
            p = jnp.exp(s_new - m)
            total = jnp.sum(p, axis=1, keepdims=True)
            out = jnp.dot(p.astype(jnp.bfloat16), value, preferred_element_type=jnp.float32)
            for s, w in chunks:
                p = jnp.exp(s - m)
                total = total + jnp.sum(p, axis=1, keepdims=True)
                out = out + jnp.dot(
                    p.astype(jnp.bfloat16), pool_v[w, pl.ds(HD, HD)], preferred_element_type=jnp.float32
                )
            out = out / total
            for g in range(GROUP):
                acc[rows, g * HD : (g + 1) * HD] = out[g * NEW : (g + 1) * NEW, :]

        @pl.when(is_long)
        def _():
            finish(6, LONG // 6)

        @pl.when(jnp.logical_not(is_long))
        def _():
            finish(1, SHORT)

        return begin + length, jnp.maximum(waited, need)

    _, waited = lax.fori_loop(0, REQ_DEV, request, (jnp.int32(0), jnp.int32(0)))

    def wait_rest(i, c):
        pool_copy(i).wait()
        return c

    lax.fori_loop(waited, NPC, wait_rest, 0)
    attn_ref[...] = acc[:, 0:QW].astype(jnp.bfloat16)
    newkv_ref[...] = acc[:, QW : QW + KW].astype(jnp.bfloat16)
    last_ref[...] = jnp.concatenate(
        [acc[r * NEW + NEW - 1 : (r + 1) * NEW, 0:QW] for r in range(REQ_DEV)], axis=0
    ).astype(jnp.bfloat16)


def attention_call(cache_len, tokens, w_query, w_keyval, query_bias, keyval_bias, gain, pool):
    vmem = pl.BlockSpec(memory_space=pltpu.VMEM)
    hbm = pl.BlockSpec(memory_space=pl.ANY)
    smem = pl.BlockSpec(memory_space=pltpu.SMEM)
    return pl.pallas_call(
        attn_kernel,
        out_shape=(
            jax.ShapeDtypeStruct((ROWS, KW), jnp.bfloat16),
            jax.ShapeDtypeStruct((ROWS, QW), jnp.bfloat16),
            jax.ShapeDtypeStruct((REQ_DEV, QW), jnp.bfloat16),
        ),
        in_specs=[smem, hbm, hbm, hbm, vmem, vmem, vmem, vmem, hbm],
        out_specs=(vmem, vmem, vmem),
        scratch_shapes=[
            pltpu.VMEM((ROWS, D), jnp.bfloat16),
            pltpu.VMEM((D, QW + KW), jnp.bfloat16),
            pltpu.VMEM((POOL, KW), jnp.bfloat16),
            pltpu.VMEM((ROWS, QW + KW), jnp.float32),
            pltpu.VMEM((ROWS, HD), jnp.float32),
            pltpu.SemaphoreType.DMA((NKC,)),
            pltpu.SemaphoreType.DMA((NKC,)),
            pltpu.SemaphoreType.DMA((NKC,)),
            pltpu.SemaphoreType.DMA((NPC,)),
        ],
        compiler_params=pltpu.CompilerParams(vmem_limit_bytes=48 * 1024 * 1024),
        name="attend",
    )(
        cache_len,
        tokens,
        w_query,
        w_keyval,
        query_bias.reshape(1, QW),
        keyval_bias.reshape(1, KW),
        gain.reshape(1, D),
        jnp.asarray(rope_tables()),
        pool,
    )


def local(
    tokens,
    w_query,
    query_bias,
    w_keyval,
    keyval_bias,
    w_out,
    attn_gain,
    final_norm_gain,
    head_weight,
    kv_pool,
    cache_len,
):
    tp_count = lax.axis_size("tp")
    tp_index = lax.axis_index("tp")
    new_kv, attention, attn_last = attention_call(
        cache_len,
        tokens,
        w_query,
        w_keyval,
        query_bias,
        keyval_bias,
        attn_gain,
        kv_pool.reshape(POOL, KW),
    )
    new_kv = new_kv.reshape(ROWS, 1, KW)
    width_local = D // tp_count
    partial_value = jnp.dot(attention, w_out, preferred_element_type=jnp.float32)
    summed = lax.psum(partial_value.astype(jnp.bfloat16), "tp").astype(jnp.float32)
    states_full = (tokens.astype(jnp.float32) + summed).astype(jnp.bfloat16)
    states = lax.dynamic_slice_in_dim(states_full, tp_index * width_local, width_local, 1)
    last_rows = states_full.reshape(REQ_DEV, NEW, D)[:, NEW - 1, :].astype(jnp.float32)
    row_norms = jnp.sqrt(jnp.mean(last_rows * last_rows, axis=1) + EPS)
    final_rows = (last_rows / row_norms[:, None] * final_norm_gain[None, :]).astype(jnp.bfloat16)
    logits = jnp.dot(
        lax.all_gather(final_rows, "req", axis=0, tiled=True),
        head_weight,
        preferred_element_type=jnp.float32,
    )
    logit_max = lax.pmax(jnp.max(logits, axis=1), ("req", "tp"))
    return (states, new_kv, row_norms, logit_max, logits)


def solution(mesh):
    return jax.shard_map(
        local,
        mesh=mesh,
        in_specs=(
            P("req", None),
            P(None, "tp"),
            P("tp"),
            P(None, "tp"),
            P("tp"),
            P("tp", None),
            P(),
            P(),
            P(None, ("req", "tp")),
            P("req", "tp", None),
            P(),
        ),
        out_specs=(P("req", "tp"), P("req", "tp", None), P("req"), P(), P(None, ("req", "tp"))),
        check_vma=False,
    )
```

time: 366 us -> 265 us (0.72)
  local copies, waits for them, and re-layouts: 69.7 us -> 9.48 us
  matrix products: 51.4 us -> 13.5 us
  other arithmetic: 28.1 us -> 6 us
  Pallas kernels: 0 us -> 20.7 us
    gather x32 -> x0, local copies, waits for them, and re-layouts: 48.3 us -> none
    dot_general x12 -> x0, matrix products: 35 us -> none  [the longest x4 16.9 us: per_request(): jnp.einsum('mjl,wml->mjw', query_block, window[..., :head_width], preferr...]
    pallas_call x0 -> x1, Pallas kernels: none -> 20.7 us  [attention_call(): pl.pallas_call(attn_kernel, out_shape=(jax.ShapeDtypeStruct((ROWS, KW), j...]
    reduce_sum x6 -> x0, other arithmetic: 8.59 us -> none  [the longest x5 5.48 us: online_update(): totals = totals * rescale + jnp.sum(weight_matrix, axis=-1)]
    convert_element_type x6 -> x2, other arithmetic: 10.8 us -> 5.03 us  [the longest x1 4.77 us: local(): states_full = (tokens.astype(jnp.float32) + summed).astype(jnp.bfloat16)]
    concatenate x6 -> x0, local copies, waits for them, and re-layouts: 4.9 us -> none  [the longest x2 4.87 us: rope_rotate(): jnp.concatenate([front_part * cosine - back_part * sine_part, back_part *...]
    sub x2 -> x0, other arithmetic: 4.17 us -> none  [the longest x1 4.16 us: rope_rotate(): front_part * cosine - back_part * sine_part]
where the time goes in v1:
time: 265 us; the launch traced here: 264 us
  waiting for transfers between devices  136 us (51%)
  blocking collectives  64.5 us (24%)
  Pallas kernels  20.7 us (8%)
  between operations  14.1 us (5%)
  matrix products  13.5 us (5%)
  local copies, waits for them, and re-layouts  9.48 us (4%)
  other arithmetic  6 us (2%)
    psum x1, waiting for transfers between devices, local(): lax.psum(partial_value.astype(jnp.bfloat16), 'tp').astype(jnp.float32)  90.6 us
    pmax x1, blocking collectives, local(): logit_max = lax.pmax(jnp.max(logits, axis=1), ('req', 'tp'))  64.5 us
    all_gather x1, waiting for transfers between devices, local(): lax.all_gather(final_rows, 'req', axis=0, tiled=True)  45.3 us
    pallas_call x1, Pallas kernels, attention_call(): pl.pallas_call(attn_kernel, out_shape=(jax.ShapeDtypeStruct((ROWS, KW), j...  20.7 us
    dot_general x1, matrix products, local(): jnp.dot(lax.all_gather(final_rows, 'req', axis=0, tiled=True), head_weigh...  8.71 us
    unnamed x18, local copies, waits for them, and re-layouts  6.57 us
  transfers between devices with their start and end apart: 2, of which 2 were waited for; matrix products, arithmetic and copies ran while one was open for 1% of the time, Pallas kernels for 0%

profile of v1, /device:TPU:0, one launch (start us, length us, event | category | flops | bytes accessed | tf_op | source)
XLA Modules:
  0.0 264.3 jit_solution(56542936146649585)
XLA Ops:
  7.2 0.0 all-reduce.2.cloned.1.call-start
  7.2 0.7 reshape.36.qb_ref
  7.9 0.0 copy-start
  7.9 1.7 copy-done
  9.6 0.0 copy-start.1
  9.6 0.8 copy-done.1
  10.4 0.0 copy-start.2
  10.4 0.7 copy-done.2
  11.2 0.0 copy-start.3
  11.2 0.7 copy-done.3
  11.9 0.7 copy-done.4
  12.5 20.7 %attend.1 = (bf16[384,256]{1,0:T(8,128)(2,1)}, bf16[384,640]{1,0:T(8,128)(2,1)S(1)}, bf16[16,640]{1,0:T(8,128)(2,1)}) custom-call(s32[512]{0:T(512)S(1)} %copy-done.3, bf16[384,5120]{1,0:T(8,128)(2,1)} %tok_hbm.1, bf16[5120,640]{1,0:T(8,128)(2,1)} %wq_hbm.1, bf16[5120,256]{1,0:T(8,128)(2,1)S(1)} %copy-done, f32[1,640]{1,0:T(1,128)S(1)} %reshape.36.qb_ref, ...), custom_call_target="tpu_custom_call" | custom-call | tf_op jit(solution)/shard_map/attend/pallas_call | solution.py:205
  33.2 0.0 copy-done.8
  33.2 4.8 %convolution_convert_fusion = bf16[384,5120]{1,0:T(8,128)(2,1)} fusion(bf16[384,640]{1,0:T(8,128)(2,1)S(1)} %get-tuple-element.7, bf16[640,5120]{1,0:T(8,128)(2,1)S(1)} %copy-done.8), kind=kOutput, calls=%fused_computation.1 | convolution fusion | flops 2518548480 | bytes 10977280 | tf_op jit(solution)/shard_map/dot_general | solution.py:267
  38.0 0.0 all-reduce.2.cloned.1.call-update
  38.0 0.0 copy-start.6
  38.0 0.0 all-gather.2.cloned.1.call-start
  38.1 90.6 %all-reduce.2.cloned.1.call-done = bf16[384,5120]{1,0:T(8,128)(2,1)} async-done(((bf16[384,5120]{1,0:T(8,128)(2,1)}), bf16[384,5120]{1,0:T(8,128)(2,1)}) %all-reduce.2.cloned.1.call-update) | async-done | bytes 3932176 | tf_op jit(solution)/shard_map/psum | solution.py:268
  128.7 4.8 %add_convert_fusion = bf16[384,5120]{1,0:T(8,128)(2,1)S(1)} fusion(bf16[384,5120]{1,0:T(8,128)(2,1)} %all-reduce.2.cloned.1.call-done, bf16[384,5120]{1,0:T(8,128)(2,1)} %tok_hbm.1), kind=kLoop, calls=%fused_computation | loop fusion | flops 7864320 | bytes 11796480 | tf_op jit(solution)/shard_map/convert_element_type | solution.py:269
  133.5 0.0 copy-start.5
  133.5 1.9 copy-done.5
  135.4 0.3 slice_convert_fusion
  135.7 0.2 fusion
  135.9 0.0 copy-done.6
  135.9 0.0 copy-start.7
  135.9 0.8 fusion.2
  136.7 0.0 all-gather.2.cloned.1.call-update
  136.7 2.2 constant_dynamic-slice_fusion
  138.9 45.3 %all-gather.2.cloned.1.call-done = bf16[512,5120]{1,0:T(8,128)(2,1)} async-done(((bf16[16,5120]{1,0:T(8,128)(2,1)}), bf16[512,5120]{1,0:T(8,128)(2,1)}) %all-gather.2.cloned.1.call-update) | async-done | bytes 5242896 | tf_op jit(solution)/shard_map/all_gather | solution.py:275
  184.2 8.7 %fusion.3 = (f32[512]{0:T(512)S(1)}, f32[512,594]{0,1:T(8,128)}) fusion(bf16[512,5120]{1,0:T(8,128)(2,1)} %all-gather.2.cloned.1.call-done, bf16[5120,594]{0,1:T(8,128)(2,1)} %param.20), kind=kOutput, calls=%fused_computation.10 | convolution fusion | flops 3114574336 | bytes 12544000 | tf_op jit(solution)/shard_map/dot_general | solution.py:274
  192.9 0.0 copy-done.7
  192.9 64.5 %pmax.7 = f32[512]{0:T(512)} all-reduce(f32[512]{0:T(512)S(1)} %get-tuple-element.9), channel_id=1, replica_groups=mesh['req'=32,'tp'=4] {'req','tp'}, use_global_device_ids=true, to_apply=%region_3.0 | all-reduce | flops 512 | bytes 4096 | tf_op jit(solution)/shard_map/pmax | solution.py:279
  (3 shorter events, 0.0 us)
Async XLA Ops:
  7.2 121.5 %all-reduce.2.cloned.1.call-start = ((), (), s32[]{:S(2)}) async-start(), calls=%async_computation | async-start | bytes 7864320 | tf_op jit(solution)/shard_map/psum | solution.py:268
  7.9 1.7 copy-start
  9.6 0.8 copy-start.1
  10.4 0.7 copy-start.2
  11.2 0.7 copy-start.3
  11.9 0.7 copy-start.4
  12.5 20.7 %copy-start.8 = (bf16[640,5120]{1,0:T(8,128)(2,1)S(1)}, bf16[640,5120]{1,0:T(8,128)(2,1)}, u32[]{:S(2)}) copy-start(bf16[640,5120]{1,0:T(8,128)(2,1)} %param.17) | copy-start | bytes 19660804
  38.0 97.8 %copy-start.6 = (f32[5120]{0:T(1024)S(1)}, f32[5120]{0:T(1024)}, u32[]{:S(2)}) copy-start(f32[5120]{0:T(1024)} %param.19) | copy-start | bytes 61444
  38.0 146.2 %all-gather.2.cloned.1.call-start = ((), (), s32[]{:S(2)}) async-start(), calls=%async_computation.1 | async-start | bytes 5406720 | tf_op jit(solution)/shard_map/all_gather | solution.py:275
  133.5 1.9 copy-start.5
  135.9 57.1 %copy-start.7 = (f32[16]{0:T(128)}, f32[16]{0:T(128)S(1)}, u32[]{:S(2)}) copy-start(f32[16]{0:T(128)S(1)} %add_sqrt_fusion) | copy-start | bytes 196
Sparse Core Ops, SparseCore 0:
  38.2 90.5 all-reduce.1
  136.8 47.3 all-gather.1

commit v2 on v1

--- a/solution.py
+++ b/solution.py
@@ -51,7 +51,6 @@
     pool_hbm,
     newkv_ref,
     attn_ref,
-    last_ref,
     tok_v,
     w_v,
     pool_v,
@@ -193,9 +192,6 @@
     lax.fori_loop(waited, NPC, wait_rest, 0)
     attn_ref[...] = acc[:, 0:QW].astype(jnp.bfloat16)
     newkv_ref[...] = acc[:, QW : QW + KW].astype(jnp.bfloat16)
-    last_ref[...] = jnp.concatenate(
-        [acc[r * NEW + NEW - 1 : (r + 1) * NEW, 0:QW] for r in range(REQ_DEV)], axis=0
-    ).astype(jnp.bfloat16)
 
 
 def attention_call(cache_len, tokens, w_query, w_keyval, query_bias, keyval_bias, gain, pool):
@@ -207,10 +203,9 @@
         out_shape=(
             jax.ShapeDtypeStruct((ROWS, KW), jnp.bfloat16),
             jax.ShapeDtypeStruct((ROWS, QW), jnp.bfloat16),
-            jax.ShapeDtypeStruct((REQ_DEV, QW), jnp.bfloat16),
         ),
         in_specs=[smem, hbm, hbm, hbm, vmem, vmem, vmem, vmem, hbm],
-        out_specs=(vmem, vmem, vmem),
+        out_specs=(vmem, vmem),
         scratch_shapes=[
             pltpu.VMEM((ROWS, D), jnp.bfloat16),
             pltpu.VMEM((D, QW + KW), jnp.bfloat16),
@@ -237,6 +232,345 @@
     )
 
 
+CHUNKS = 4
+CROWS = ROWS // CHUNKS
+HROWS = CROWS // 2
+TP = 4
+WIDTH = D // TP
+NT = 256
+HALF = D // 2
+QUART = HALF // 2
+VLOC = 594
+GROUP_ROWS = 128
+MESH = pl.DeviceIdType.MESH
+N_COPIES = 112
+
+
+def tail_kernel(
+    attn_ref,
+    gain_ref,
+    tok_hbm,
+    wo_hbm,
+    hw_hbm,
+    states_ref,
+    norms_ref,
+    max_ref,
+    logits_ref,
+    tok_v,
+    wo_v,
+    hw_v,
+    gathered,
+    final,
+    last_out,
+    last_in,
+    far_out,
+    far_l,
+    far_r,
+    part_r,
+    part_l,
+    part_own,
+    near_out_r,
+    near_out_l,
+    near_in_l,
+    near_in_r,
+    mx,
+    mx_in,
+    tok_sem,
+    wo_sem,
+    hw_sem,
+    send_sem,
+    recv_sem,
+):
+    req = lax.axis_index("req")
+    y = lax.axis_index("tp")
+    core = lax.rem(req, 2)
+    x = lax.rem(req // 2, 4)
+    z = req // 8
+    right, left, opp = lax.rem(y + 1, TP), lax.rem(y + 3, TP), lax.rem(y + 2, TP)
+
+    def at(dx=0, dz=0, dc=0, dy=0):
+        xx, zz, cc = lax.rem(x + dx, 4), lax.rem(z + dz, 4), lax.rem(core + dc, 2)
+        return {"req": (zz * 4 + xx) * 2 + cc, "tp": lax.rem(y + dy, TP)}
+
+    peers = [at(dx=1), at(dx=2), at(dx=3), at(dz=1), at(dz=2), at(dz=3), at(dy=1), at(dy=2), at(dy=3), at(dc=1)]
+
+    def wide(d):
+        return pl.ds(pl.multiple_of(d * WIDTH, WIDTH), WIDTH)
+
+    tok_copy = pltpu.make_async_copy(tok_hbm.at[:, wide(y)], tok_v, tok_sem)
+    hw_copy = pltpu.make_async_copy(hw_hbm, hw_v, hw_sem)
+    wo_copies = {}
+    for i, d in enumerate((opp, right, left, y)):
+        wo_copies[i] = pltpu.make_async_copy(wo_hbm.at[:, wide(d)], wo_v.at[i], wo_sem.at[i])
+        wo_copies[i].start()
+    tok_copy.start()
+    hw_copy.start()
+
+    barrier = pltpu.get_barrier_semaphore()
+    for peer in peers:
+        pl.semaphore_signal(barrier, inc=1, device_id=peer, device_id_type=MESH)
+    pl.semaphore_wait(barrier, len(peers))
+
+    copies = {}
+
+    def send(name, src, dst, device):
+        i = len(copies)
+        copies[name] = pltpu.make_async_remote_copy(
+            src_ref=src,
+            dst_ref=dst,
+            send_sem=send_sem.at[i],
+            recv_sem=recv_sem.at[i],
+            device_id=device,
+            device_id_type=MESH,
+        )
+        copies[name].start()
+
+    def got(name):
+        copies[name].wait_recv()
+
+    pick_row = lax.broadcasted_iota(jnp.int32, (REQ_DEV, ROWS), 0)
+    pick_col = lax.broadcasted_iota(jnp.int32, (REQ_DEV, ROWS), 1)
+    pick = (pick_col == pick_row * NEW + (NEW - 1)).astype(jnp.bfloat16)
+    attn_last = jnp.dot(pick, attn_ref[...], preferred_element_type=jnp.float32).astype(jnp.bfloat16)
+
+    for i, dy in enumerate((2, 1, 3)):
+        wo_copies[i].wait()
+        last_out[i] = jnp.dot(attn_last, wo_v[i], preferred_element_type=jnp.float32).astype(jnp.bfloat16)
+        send(("last", dy), last_out.at[i], last_in.at[i], at(dy=dy))
+    wo_copies[3].wait()
+
+    def project(i, out_ref):
+        @pl.loop(0, WIDTH // NT)
+        def _(t):
+            c = pl.ds(pl.multiple_of(t * NT, NT), NT)
+            out_ref[:, c] = jnp.dot(
+                attn_ref[...], wo_v[i, :, c], preferred_element_type=jnp.float32
+            ).astype(out_ref.dtype)
+
+    def far_send(c):
+        r = c * CROWS
+        send(("far", c, 1), far_out.at[r : r + HROWS], far_l.at[c], at(dy=1))
+        send(("far", c, 3), far_out.at[r + HROWS : r + CROWS], far_r.at[c], at(dy=3))
+
+    own_last = jnp.dot(attn_last, wo_v[3], preferred_element_type=jnp.float32)
+    project(0, far_out)
+    far_send(0)
+    tok_copy.wait()
+    own_last = own_last + jnp.dot(pick, tok_v[...], preferred_element_type=jnp.float32)
+    for i, dy in enumerate((2, 1, 3)):
+        got(("last", dy))
+        own_last = own_last + last_in[i].astype(jnp.float32)
+    own_rows = pl.ds(pl.multiple_of(req * REQ_DEV, REQ_DEV), REQ_DEV)
+    gathered[own_rows, wide(y)] = own_last.astype(jnp.bfloat16)
+    for dy in (1, 3, 2):
+        block = gathered.at[own_rows, wide(y)]
+        send(("slice", dy), block, block, at(dy=dy))
+    far_send(1)
+    project(1, part_r)
+    project(2, part_l)
+    for dy in (1, 3, 2):
+        got(("slice", dy))
+
+    def device(half, df=0, ds=0):
+        return at(dx=df, dz=ds) if half == 0 else at(dx=ds, dz=df)
+
+    def piece(half, df, ds, part=None):
+        d = device(half, df, ds)["req"]
+        rows = pl.ds(pl.multiple_of(d * REQ_DEV, REQ_DEV), REQ_DEV)
+        start, width = half * HALF, HALF
+        if part is not None:
+            start, width = start + part * QUART, QUART
+        return gathered.at[rows, start : start + width]
+
+    def push(name, half, df, ds, to, part=None):
+        block = piece(half, df, ds, part)
+        send((name, half, df, ds, part), block, block, to)
+
+    def spread(half, k):
+        for side in (1, 3):
+            block = piece(half, k, 0)
+            send(("second", half, k, side), block, block, device(half, 0, side))
+
+    def sibling(half, df, ds):
+        push("sib", half, df, ds, at(dc=1))
+
+    for half in (0, 1):
+        for side in (1, 3):
+            block = piece(half, 0, 0)
+            send(("first", half, side), block, block, device(half, side, 0))
+    for half in (0, 1):
+        spread(half, 0)
+    for half in (0, 1):
+        sibling(half, 0, 0)
+
+    own_state = gathered[own_rows, :].astype(jnp.float32)
+    own_norm = jnp.sqrt(jnp.sum(own_state * own_state, axis=1, keepdims=True) * (1.0 / D) + EPS)
+    eye_row = lax.broadcasted_iota(jnp.int32, (REQ_DEV, REQ_DEV), 0)
+    eye_col = lax.broadcasted_iota(jnp.int32, (REQ_DEV, REQ_DEV), 1)
+    norms_ref[...] = jnp.sum(jnp.where(eye_row == eye_col, own_norm, 0.0), axis=0, keepdims=True)
+
+    def near_step(c):
+        r = c * CROWS
+        got(("far", c, 1))
+        near_out_r[c, 0:HROWS] = (part_r[r : r + HROWS] + far_l[c].astype(jnp.float32)).astype(jnp.bfloat16)
+        near_out_r[c, HROWS:CROWS] = part_r[r + HROWS : r + CROWS].astype(jnp.bfloat16)
+        send(("near", c, 1), near_out_r.at[c], near_in_l.at[c], at(dy=1))
+        got(("far", c, 3))
+        near_out_l[c, 0:HROWS] = part_l[r : r + HROWS].astype(jnp.bfloat16)
+        near_out_l[c, HROWS:CROWS] = (part_l[r + HROWS : r + CROWS] + far_r[c].astype(jnp.float32)).astype(jnp.bfloat16)
+        send(("near", c, 3), near_out_l.at[c], near_in_r.at[c], at(dy=3))
+
+    def relay_second(half, k):
+        for side, part, ds in ((1, 0, 3), (3, 1, 1)):
+            got(("second", half, k, side))
+            block = piece(half, k, ds, part)
+            send(("third", half, k, side), block, block, device(half, 0, side))
+            sibling(half, k, ds)
+
+    def finish_second(half, k):
+        for side in (1, 3):
+            got(("third", half, k, side))
+        sibling(half, k, 2)
+
+    def logits_of(dz):
+        zz = lax.rem(z + dz, 4)
+        for dx in range(4):
+            got(("sib", 0, dx, dz, None))
+            got(("sib", 1, dz, dx, None))
+
+        @pl.loop(0, GROUP_ROWS // REQ_DEV)
+        def _(t):
+            src = pl.ds(pl.multiple_of(zz * GROUP_ROWS + t * REQ_DEV, REQ_DEV), REQ_DEV)
+            g = gathered[src, :].astype(jnp.float32)
+            inv = 1.0 / jnp.sqrt(jnp.sum(g * g, axis=1, keepdims=True) * (1.0 / D) + EPS)
+            dst = pl.ds(pl.multiple_of(t * REQ_DEV, REQ_DEV), REQ_DEV)
+            final[dst, :] = (g * inv * gain_ref[...]).astype(jnp.bfloat16)
+
+        out = lax.dot_general(
+            hw_v[...], final[...], (((1,), (1,)), ((), ())), preferred_element_type=jnp.float32
+        )
+        logits_ref[:, pl.ds(pl.multiple_of(zz * GROUP_ROWS, GROUP_ROWS), GROUP_ROWS)] = out
+        mx[0, pl.ds(zz, 1), :] = jnp.max(out, axis=0, keepdims=True)
+
+    far_send(2)
+    far_send(3)
+    for half in (0, 1):
+        for side, part, df in ((1, 0, 3), (3, 1, 1)):
+            got(("first", half, side))
+            block = piece(half, df, 0, part)
+            send(("relay", half, side), block, block, device(half, side, 0))
+            spread(half, df)
+            sibling(half, df, 0)
+    near_step(0)
+    for half in (0, 1):
+        relay_second(half, 0)
+    for half in (0, 1):
+        for side in (1, 3):
+            got(("relay", half, side))
+        spread(half, 2)
+        sibling(half, 2, 0)
+    near_step(1)
+    project(3, part_own)
+    for k in (3, 1):
+        for half in (0, 1):
+            relay_second(half, k)
+    near_step(2)
+    for half in (0, 1):
+        finish_second(half, 0)
+    near_step(3)
+    hw_copy.wait()
+    logits_of(0)
+    for half in (0, 1):
+        relay_second(half, 2)
+    for k in (3, 1):
+        for half in (0, 1):
+            finish_second(half, k)
+    logits_of(1)
+    logits_of(3)
+    for half in (0, 1):
+        finish_second(half, 2)
+    logits_of(2)
+
+    def spread_max(stage, moves):
+        for i, move in enumerate(moves):
+            send(("max", stage, i), mx.at[stage], mx_in.at[stage, i], at(**move))
+
+    def take_max(stage, moves):
+        m = mx[stage]
+        for i in range(len(moves)):
+            got(("max", stage, i))
+            m = jnp.maximum(m, mx_in[stage, i])
+        return m
+
+    stages = [
+        [{"dc": 1}],
+        [{"dx": 1}, {"dx": 3}, {"dx": 2}],
+        [{"dz": 1}, {"dz": 3}, {"dz": 2}],
+        [{"dy": 1}, {"dy": 3}, {"dy": 2}],
+    ]
+    for s in range(3):
+        spread_max(s, stages[s])
+        mx[s + 1] = take_max(s, stages[s])
+    spread_max(3, stages[3])
+
+    for c in range(CHUNKS):
+        r = slice(c * CROWS, (c + 1) * CROWS)
+        got(("near", c, 1))
+        got(("near", c, 3))
+        total = tok_v[r].astype(jnp.float32) + part_own[r] + near_in_l[c].astype(jnp.float32)
+        states_ref[r] = (total + near_in_r[c].astype(jnp.float32)).astype(jnp.bfloat16)
+    max_ref[...] = take_max(3, stages[3])
+    for c in copies.values():
+        c.wait_send()
+
+
+def tail_call(attention, gain, tokens, w_out, head_t):
+    vmem = pl.BlockSpec(memory_space=pltpu.VMEM)
+    hbm = pl.BlockSpec(memory_space=pl.ANY)
+    half = jnp.bfloat16
+    return pl.pallas_call(
+        tail_kernel,
+        out_shape=(
+            jax.ShapeDtypeStruct((ROWS, WIDTH), half),
+            jax.ShapeDtypeStruct((1, REQ_DEV), jnp.float32),
+            jax.ShapeDtypeStruct((4, GROUP_ROWS), jnp.float32),
+            jax.ShapeDtypeStruct((VLOC, 4 * GROUP_ROWS), jnp.float32),
+        ),
+        in_specs=[vmem, vmem, hbm, hbm, hbm],
+        out_specs=(vmem, vmem, vmem, vmem),
+        scratch_shapes=[
+            pltpu.VMEM((ROWS, WIDTH), half),
+            pltpu.VMEM((TP, QW, WIDTH), half),
+            pltpu.VMEM((VLOC, D), half),
+            pltpu.VMEM((4 * GROUP_ROWS, D), half),
+            pltpu.VMEM((GROUP_ROWS, D), half),
+            pltpu.VMEM((3, REQ_DEV, WIDTH), half),
+            pltpu.VMEM((3, REQ_DEV, WIDTH), half),
+            pltpu.VMEM((ROWS, WIDTH), half),
+            pltpu.VMEM((CHUNKS, HROWS, WIDTH), half),
+            pltpu.VMEM((CHUNKS, HROWS, WIDTH), half),
+            pltpu.VMEM((ROWS, WIDTH), jnp.float32),
+            pltpu.VMEM((ROWS, WIDTH), jnp.float32),
+            pltpu.VMEM((ROWS, WIDTH), jnp.float32),
+            pltpu.VMEM((CHUNKS, CROWS, WIDTH), half),
+            pltpu.VMEM((CHUNKS, CROWS, WIDTH), half),
+            pltpu.VMEM((CHUNKS, CROWS, WIDTH), half),
+            pltpu.VMEM((CHUNKS, CROWS, WIDTH), half),
+            pltpu.VMEM((4, 4, GROUP_ROWS), jnp.float32),
+            pltpu.VMEM((4, 3, 4, GROUP_ROWS), jnp.float32),
+            pltpu.SemaphoreType.DMA,
+            pltpu.SemaphoreType.DMA((TP,)),
+            pltpu.SemaphoreType.DMA,
+            pltpu.SemaphoreType.DMA((N_COPIES,)),
+            pltpu.SemaphoreType.DMA((N_COPIES,)),
+        ],
+        compiler_params=pltpu.CompilerParams(
+            vmem_limit_bytes=52 * 1024 * 1024, collective_id=0, has_side_effects=True
+        ),
+        name="tail",
+    )(attention, gain.reshape(1, D), tokens, w_out, head_t)
+
+
 def local(
     tokens,
     w_query,
@@ -250,9 +584,7 @@
     kv_pool,
     cache_len,
 ):
-    tp_count = lax.axis_size("tp")
-    tp_index = lax.axis_index("tp")
-    new_kv, attention, attn_last = attention_call(
+    new_kv, attention = attention_call(
         cache_len,
         tokens,
         w_query,
@@ -262,22 +594,14 @@
         attn_gain,
         kv_pool.reshape(POOL, KW),
     )
-    new_kv = new_kv.reshape(ROWS, 1, KW)
-    width_local = D // tp_count
-    partial_value = jnp.dot(attention, w_out, preferred_element_type=jnp.float32)
-    summed = lax.psum(partial_value.astype(jnp.bfloat16), "tp").astype(jnp.float32)
-    states_full = (tokens.astype(jnp.float32) + summed).astype(jnp.bfloat16)
-    states = lax.dynamic_slice_in_dim(states_full, tp_index * width_local, width_local, 1)
-    last_rows = states_full.reshape(REQ_DEV, NEW, D)[:, NEW - 1, :].astype(jnp.float32)
-    row_norms = jnp.sqrt(jnp.mean(last_rows * last_rows, axis=1) + EPS)
-    final_rows = (last_rows / row_norms[:, None] * final_norm_gain[None, :]).astype(jnp.bfloat16)
-    logits = jnp.dot(
-        lax.all_gather(final_rows, "req", axis=0, tiled=True),
-        head_weight,
-        preferred_element_type=jnp.float32,
+    states, norms, top, logits_t = tail_call(attention, final_norm_gain, tokens, w_out, head_weight.T)
+    return (
+        states,
+        new_kv.reshape(ROWS, 1, KW),
+        norms.reshape(REQ_DEV),
+        top.reshape(4 * GROUP_ROWS),
+        logits_t.T,
     )
-    logit_max = lax.pmax(jnp.max(logits, axis=1), ("req", "tp"))
-    return (states, new_kv, row_norms, logit_max, logits)
 
 
 def solution(mesh):

time: 265 us -> 98.6 us (0.37)
  waiting for transfers between devices: 136 us -> 0 us
  Pallas kernels: 20.7 us -> 87.8 us
  blocking collectives: 64.5 us -> 0 us
  matrix products: 13.5 us -> 0 us
  between operations: 14.1 us -> 0.66 us
  other arithmetic: 6 us -> 0 us
    psum x1 -> x0, waiting for transfers between devices: 90.6 us -> none  [local(): lax.psum(partial_value.astype(jnp.bfloat16), 'tp').astype(jnp.float32)]
    pallas_call x0 -> x1, Pallas kernels: none -> 70.6 us  [tail_call(): pl.pallas_call(tail_kernel, out_shape=(jax.ShapeDtypeStruct((ROWS, WIDTH)...]
    pmax x1 -> x0, blocking collectives: 64.5 us -> none  [local(): logit_max = lax.pmax(jnp.max(logits, axis=1), ('req', 'tp'))]
    all_gather x1 -> x0, waiting for transfers between devices: 45.3 us -> none  [local(): lax.all_gather(final_rows, 'req', axis=0, tiled=True)]
    dot_general x2 -> x0, matrix products: 13.5 us -> none  [the longest x1 8.71 us: local(): jnp.dot(lax.all_gather(final_rows, 'req', axis=0, tiled=True), head_weigh...]
    convert_element_type x3 -> x0, other arithmetic: 5.82 us -> none  [the longest x1 4.77 us: local(): states_full = (tokens.astype(jnp.float32) + summed).astype(jnp.bfloat16)]
    pallas_call x1, Pallas kernels: 20.7 us -> 17.2 us  [attention_call(): pl.pallas_call(attn_kernel, out_shape=(jax.ShapeDtypeStruct((ROWS, KW), j...]
    unnamed x18 -> x16, local copies, waits for them, and re-layouts: 6.57 us -> 9.06 us
  transfers between devices with their start and end apart: 2 -> 0, of which waited for: 2 -> 0; matrix products, arithmetic and copies ran while one was open for 1% -> 0% of each run, Pallas kernels for 0% -> 0%
where the time goes in v2:
time: 98.6 us; the launch traced here: 98.3 us
  Pallas kernels  87.8 us (89%)
  local copies, waits for them, and re-layouts  9.75 us (10%)
    pallas_call x1, Pallas kernels, tail_call(): pl.pallas_call(tail_kernel, out_shape=(jax.ShapeDtypeStruct((ROWS, WIDTH)...  70.6 us
    pallas_call x1, Pallas kernels, attention_call(): pl.pallas_call(attn_kernel, out_shape=(jax.ShapeDtypeStruct((ROWS, KW), j...  17.2 us
    unnamed x16, local copies, waits for them, and re-layouts  9.06 us

profile of v2, /device:TPU:0, one launch (start us, length us, event | category | flops | bytes accessed | tf_op | source)
XLA Modules:
  0.0 98.3 jit_solution(5126205286488435540)
XLA Ops:
  0.6 0.7 reshape.34.qb_ref
  1.3 0.0 copy-start
  1.3 1.7 %copy-done = bf16[5120,256]{1,0:T(8,128)(2,1)S(1)} copy-done((bf16[5120,256]{1,0:T(8,128)(2,1)S(1)}, bf16[5120,256]{1,0:T(8,128)(2,1)}, u32[]{:S(2)}) %copy-start) | copy-done | bytes 2621464
  3.1 0.0 copy-start.1
  3.1 0.8 copy-done.1
  3.9 0.0 copy-start.2
  3.9 0.7 copy-done.2
  4.6 0.0 copy-start.4
  4.6 0.7 copy-done.4
  5.3 0.0 copy-start.5
  5.3 0.7 copy-done.5
  6.0 0.0 copy-start.3
  6.0 17.2 %attend.1 = (bf16[384,256]{1,0:T(8,128)(2,1)}, bf16[384,640]{1,0:T(8,128)(2,1)S(1)}) custom-call(s32[512]{0:T(512)S(1)} %copy-done.4, bf16[384,5120]{1,0:T(8,128)(2,1)} %tok_hbm.3, bf16[5120,640]{1,0:T(8,128)(2,1)} %wq_hbm.1, bf16[5120,256]{1,0:T(8,128)(2,1)S(1)} %copy-done, f32[1,640]{1,0:T(1,128)S(1)} %reshape.34.qb_ref, f32[1,256]{1,0:T(1,128)S(1)} %bitcast.12, ...), custom_call_target="tpu_custom_call" | custom-call | tf_op jit(solution)/shard_map/attend/pallas_call | solution.py:201
  23.2 0.0 copy-done.3
  23.2 70.6 %tail.1 = (bf16[384,1280]{1,0:T(8,128)(2,1)S(1)}, f32[1,16]{1,0:T(1,128)S(1)}, f32[4,128]{1,0:T(4,128)S(1)}, f32[594,512]{1,0:T(8,128)}) custom-call(bf16[384,640]{1,0:T(8,128)(2,1)S(1)} %get-tuple-element.11.attn_ref, f32[1,5120]{1,0:T(1,128)S(1)} %bitcast.10, bf16[384,5120]{1,0:T(8,128)(2,1)} %tok_hbm.3, bf16[640,5120]{1,0:T(8,128)(2,1)} %wo_hbm.1, ...), custom_call_target="tpu_custom_call" | custom-call | tf_op jit(solution)/shard_map/tail/pallas_call | solution.py:531
  93.8 0.9 copy.21
  94.8 0.5 copy.22
  95.3 0.6 copy.23
  95.9 2.4 %copy.24 = f32[512,594]{0,1:T(8,128)} copy(f32[512,594]{0,1:T(8,128)} %bitcast.16) | data formatting | bytes 2433024
Async XLA Ops:
  1.3 1.7 %copy-start = (bf16[5120,256]{1,0:T(8,128)(2,1)S(1)}, bf16[5120,256]{1,0:T(8,128)(2,1)}, u32[]{:S(2)}) copy-start(bf16[5120,256]{1,0:T(8,128)(2,1)} %wkv_hbm.1) | copy-start | bytes 7864324
  3.1 0.8 copy-start.1
  3.9 0.7 copy-start.2
  4.6 0.7 copy-start.4
  5.3 0.7 copy-start.5
  6.0 17.3 %copy-start.3 = (f32[5120]{0:T(1024)S(1)}, f32[5120]{0:T(1024)}, u32[]{:S(2)}) copy-start(f32[5120]{0:T(1024)} %param.19) | copy-start | bytes 61444

commit v3 on v2

v3 whole, which is shorter than its diff:
```python
import math

import jax
import jax.numpy as jnp
import numpy as np
from jax import lax
from jax.experimental import pallas as pl
from jax.experimental.pallas import tpu as pltpu
from jax.sharding import PartitionSpec as P

D = 5120
HD = 128
GROUP = 5
NEW = 24
SHORT = 256
LONG = 3072
REQ_DEV = 16
REQUESTS = 512
POOL = 26624
ROWS = REQ_DEV * NEW
QW = GROUP * HD
KW = 2 * HD
THETA = 1000000.0
EPS = 1e-06
NEG = -1e30

KC = 1024
NKC = D // KC
PC = 2048
NPC = POOL // PC
QR = 128
PER_STEP = 4
BATCH = 4
WIDE = (LONG - SHORT) // 2
VLOC = 594


def rope_tables():
    freq = np.float32(THETA) ** (-(np.arange(HD // 2, dtype=np.float32) * np.float32(2.0 / HD)))
    pos = np.concatenate([SHORT + np.arange(NEW), LONG + np.arange(NEW)]).astype(np.float32)
    ang = (pos[:, None] * freq[None, :].astype(np.float32)).astype(np.float64)
    cos = np.cos(ang).astype(np.float32)
    sin = np.sin(ang).astype(np.float32)
    return np.concatenate([cos, cos, -sin, sin], axis=1)


def attn_kernel(
    lens_hbm,
    tok_hbm,
    wq_hbm,
    wkv_hbm,
    qb_hbm,
    kvb_hbm,
    gain_hbm,
    cs_hbm,
    pool_hbm,
    wo_hbm,
    hw_hbm,
    newkv_ref,
    attn_ref,
    wo_ref,
    hw_ref,
    tok_v,
    w_v,
    pool_v,
    acc,
    ss,
    att_s,
    kv_s,
    q_s,
    m_s,
    l_s,
    o_s,
    lens_ref,
    start_ref,
    long_ref,
    qb_v,
    kvb_v,
    gain_v,
    cs_ref,
    tok_sem,
    wq_sem,
    wkv_sem,
    pool_sem,
    small_sem,
    tail_sem,
):
    def tok_copy(k):
        c = pl.ds(pl.multiple_of(k * KC, KC), KC)
        return pltpu.make_async_copy(tok_hbm.at[:, c], tok_v.at[:, c], tok_sem.at[k])

    def wq_copy(k):
        c = pl.ds(pl.multiple_of(k * KC, KC), KC)
        return pltpu.make_async_copy(wq_hbm.at[c, :], w_v.at[c, pl.ds(0, QW)], wq_sem.at[k])

    def wkv_copy(k):
        c = pl.ds(pl.multiple_of(k * KC, KC), KC)
        return pltpu.make_async_copy(wkv_hbm.at[c, :], w_v.at[c, pl.ds(QW, KW)], wkv_sem.at[k])

    def pool_copy(k):
        c = pl.ds(pl.multiple_of(k * PC, PC), PC)
        return pltpu.make_async_copy(pool_hbm.at[c, :], pool_v.at[c, :], pool_sem.at[k])

    smalls = [
        pltpu.make_async_copy(src, dst, small_sem.at[i])
        for i, (src, dst) in enumerate(
            ((gain_hbm, gain_v), (lens_hbm, lens_ref), (qb_hbm, qb_v), (kvb_hbm, kvb_v), (cs_hbm, cs_ref))
        )
    ]
    tails = [
        pltpu.make_async_copy(wo_hbm, wo_ref, tail_sem.at[0]),
        pltpu.make_async_copy(hw_hbm, hw_ref, tail_sem.at[1]),
    ]
    smalls[0].start()
    smalls[1].start()
    for k in range(NKC):
        tok_copy(k).start()
        wq_copy(k).start()
        wkv_copy(k).start()
    for c in smalls[2:]:
        c.start()
    ss[...] = jnp.zeros_like(ss)
    acc[...] = jnp.zeros_like(acc)
    base = lax.axis_index("req") * REQ_DEV
    smalls[1].wait()

    def place(r, carry):
        begin, n_long = carry
        length = lens_ref[base + r]
        start_ref[r] = begin
        long_ref[n_long] = r
        return begin + length, n_long + jnp.where(length > SHORT, 1, 0)

    _, n_long = lax.fori_loop(0, REQ_DEV, place, (jnp.int32(0), jnp.int32(0)))
    smalls[0].wait()

    for k in range(NKC):
        tok_copy(k).wait()
        wq_copy(k).wait()
        wkv_copy(k).wait()
        if k >= 1:
            for i in range(PER_STEP * (k - 1), min(PER_STEP * k, NPC)):
                pool_copy(i).start()
        c = slice(k * KC, (k + 1) * KC)
        x = tok_v[:, c].astype(jnp.float32)
        sq = x * x
        part = sq[:, 0:HD]
        for i in range(1, KC // HD):
            part = part + sq[:, i * HD : (i + 1) * HD]
        ss[...] += part
        xg = (x * gain_v[c].reshape(1, KC)).astype(jnp.bfloat16)
        acc[...] += jnp.dot(xg, w_v[c, :], preferred_element_type=jnp.float32)
    for c in tails:
        c.start()

    for c in smalls[2:]:
        c.wait()
    rstd = 1.0 / jnp.sqrt(jnp.sum(ss[...], axis=1, keepdims=True) * (1.0 / D) + EPS)
    ss[...] = jnp.broadcast_to(rstd, ss.shape)

    row = lax.broadcasted_iota(jnp.int32, (QR, HD), 0)
    col = lax.broadcasted_iota(jnp.int32, (QR, HD), 1)
    token = row
    for g in range(1, GROUP + 1):
        token = token - jnp.where(row >= g * NEW, NEW, 0)
    causal = (col <= token) & (col < NEW)
    scale = 1.0 / math.sqrt(HD)

    def wait_one(i, c):
        pool_copy(i).wait()
        return c

    def scores_of(q, k):
        return lax.dot_general(q, k, (((1,), (1,)), ((), ())), preferred_element_type=jnp.float32)

    def mix(p, v):
        return jnp.dot(p.astype(jnp.bfloat16), v, preferred_element_type=jnp.float32)

    def rows_of(r):
        return pl.ds(pl.multiple_of(r * NEW, 8), NEW)

    def store_heads(r, out):
        for g in range(GROUP):
            att_s[rows_of(r), g * HD : (g + 1) * HD] = out[g * NEW : (g + 1) * NEW, :]

    def batch(b, waited):
        ids = [b * BATCH + i for i in range(BATCH)]
        begins = [start_ref[r] for r in ids]
        need = (begins[-1] + SHORT + (PC - 1)) // PC
        lax.fori_loop(waited, need, wait_one, 0)
        fill = jnp.zeros((HD - NEW, HD), jnp.float32)
        qs, keys, values = [], [], []
        for r in ids:
            rows = rows_of(r)
            table = pl.ds(pl.multiple_of(jnp.where(lens_ref[base + r] > SHORT, NEW, 0), 8), NEW)
            cos = cs_ref[table, pl.ds(0, HD)]
            sin = cs_ref[table, pl.ds(HD, HD)]
            rs = ss[rows, :]

            def rope(v, cos=cos, sin=sin):
                return v * cos + pltpu.roll(v, HD // 2, 1) * sin

            heads = []
            for g in range(GROUP):
                c = slice(g * HD, (g + 1) * HD)
                heads.append(rope(acc[rows, c] * rs + qb_v[c].reshape(1, HD)) * scale)
            heads.append(jnp.zeros((QR - GROUP * NEW, HD), jnp.float32))
            qs.append(jnp.concatenate(heads, axis=0).astype(jnp.bfloat16))
            key = rope(acc[rows, QW : QW + HD] * rs + kvb_v[0:HD].reshape(1, HD))
            value = acc[rows, QW + HD : QW + KW] * rs + kvb_v[HD:KW].reshape(1, HD)
            kv_s[rows, 0:HD] = key
            kv_s[rows, HD:KW] = value
            keys.append(jnp.concatenate([key, fill], axis=0).astype(jnp.bfloat16))
            values.append(jnp.concatenate([value, fill], axis=0).astype(jnp.bfloat16))
        windows = [pl.ds(pl.multiple_of(x, SHORT), SHORT) for x in begins]
        old = [scores_of(q, pool_v[w, pl.ds(0, HD)]) for q, w in zip(qs, windows)]
        new = [jnp.where(causal, scores_of(q, k), NEG) for q, k in zip(qs, keys)]
        ms = [
            jnp.maximum(jnp.max(s, axis=1, keepdims=True), jnp.max(t, axis=1, keepdims=True))
            for s, t in zip(old, new)
        ]
        p_old = [jnp.exp(s - m) for s, m in zip(old, ms)]
        p_new = [jnp.exp(t - m) for t, m in zip(new, ms)]
        ls = [
            jnp.sum(p, axis=1, keepdims=True) + jnp.sum(u, axis=1, keepdims=True)
            for p, u in zip(p_old, p_new)
        ]
        outs = [
            mix(p, pool_v[w, pl.ds(HD, HD)]) + mix(u, v)
            for p, u, w, v in zip(p_old, p_new, windows, values)
        ]
        for i, r in enumerate(ids):
            q_s[r] = qs[i]
            m_s[r] = jnp.broadcast_to(ms[i], (QR, HD))
            l_s[r] = jnp.broadcast_to(ls[i], (QR, HD))
            o_s[r] = outs[i]
            store_heads(r, outs[i] / ls[i])
        return jnp.maximum(waited, need)

    waited = lax.fori_loop(0, REQ_DEV // BATCH, batch, jnp.int32(0))
    lax.fori_loop(waited, NPC, wait_one, 0)

    def longs(j, carry):
        ids = [long_ref[2 * j], long_ref[jnp.minimum(2 * j + 1, n_long - 1)]]
        begins = [pl.multiple_of(start_ref[r] + SHORT, SHORT) for r in ids]
        qs = [q_s[r] for r in ids]
        windows = [
            [pl.ds(pl.multiple_of(x + i * WIDE, HD), WIDE) for i in range((LONG - SHORT) // WIDE)] for x in begins
        ]
        scores = [[scores_of(q, pool_v[w, pl.ds(0, HD)]) for w in ws] for q, ws in zip(qs, windows)]
        outs = []
        for r, ws, parts in zip(ids, windows, scores):
            before = m_s[r][:, 0:1]
            m = before
            for s in parts:
                m = jnp.maximum(m, jnp.max(s, axis=1, keepdims=True))
            fade = jnp.exp(before - m)
            total = l_s[r][:, 0:1] * fade
            out = o_s[r] * fade
            for s, w in zip(parts, ws):
                p = jnp.exp(s - m)
                total = total + jnp.sum(p, axis=1, keepdims=True)
                out = out + mix(p, pool_v[w, pl.ds(HD, HD)])
            outs.append(out / total)
        for r, out in zip(ids, outs):
            store_heads(r, out)
        return carry

    lax.fori_loop(0, (n_long + 1) // 2, longs, 0)
    attn_ref[...] = att_s[...].astype(jnp.bfloat16)
    newkv_ref[...] = kv_s[...].astype(jnp.bfloat16)
    for c in tails:
        c.wait()


def in_hbm(a):
    return pltpu.with_memory_space_constraint(a, pltpu.HBM)


def attention_call(cache_len, tokens, w_query, w_keyval, query_bias, keyval_bias, gain, pool, w_out, head_t):
    vmem = pl.BlockSpec(memory_space=pltpu.VMEM)
    hbm = pl.BlockSpec(memory_space=pltpu.HBM)
    return pl.pallas_call(
        attn_kernel,
        out_shape=(
            jax.ShapeDtypeStruct((ROWS, KW), jnp.bfloat16),
            jax.ShapeDtypeStruct((ROWS, QW), jnp.bfloat16),
            jax.ShapeDtypeStruct((QW, D), jnp.bfloat16),
            jax.ShapeDtypeStruct((VLOC, D), jnp.bfloat16),
        ),
        in_specs=[hbm] * 11,
        out_specs=(vmem, vmem, vmem, vmem),
        scratch_shapes=[
            pltpu.VMEM((ROWS, D), jnp.bfloat16),
            pltpu.VMEM((D, QW + KW), jnp.bfloat16),
            pltpu.VMEM((POOL, KW), jnp.bfloat16),
            pltpu.VMEM((ROWS, QW + KW), jnp.float32),
            pltpu.VMEM((ROWS, HD), jnp.float32),
            pltpu.VMEM((ROWS, QW), jnp.float32),
            pltpu.VMEM((ROWS, KW), jnp.float32),
            pltpu.VMEM((REQ_DEV, QR, HD), jnp.bfloat16),
            pltpu.VMEM((REQ_DEV, QR, HD), jnp.float32),
            pltpu.VMEM((REQ_DEV, QR, HD), jnp.float32),
            pltpu.VMEM((REQ_DEV, QR, HD), jnp.float32),
            pltpu.SMEM((REQUESTS,), jnp.int32),
            pltpu.SMEM((REQ_DEV,), jnp.int32),
            pltpu.SMEM((REQ_DEV + 1,), jnp.int32),
            pltpu.VMEM((QW,), jnp.float32),
            pltpu.VMEM((KW,), jnp.float32),
            pltpu.VMEM((D,), jnp.float32),
            pltpu.VMEM((2 * NEW, 2 * HD), jnp.float32),
            pltpu.SemaphoreType.DMA((NKC,)),
            pltpu.SemaphoreType.DMA((NKC,)),
            pltpu.SemaphoreType.DMA((NKC,)),
            pltpu.SemaphoreType.DMA((NPC,)),
            pltpu.SemaphoreType.DMA((5,)),
            pltpu.SemaphoreType.DMA((2,)),
        ],
        compiler_params=pltpu.CompilerParams(vmem_limit_bytes=36 * 1024 * 1024),
        name="attend",
    )(
        in_hbm(cache_len),
        in_hbm(tokens),
        in_hbm(w_query),
        in_hbm(w_keyval),
        in_hbm(query_bias),
        in_hbm(keyval_bias),
        in_hbm(gain),
        in_hbm(jnp.asarray(rope_tables())),
        in_hbm(pool),
        in_hbm(w_out),
        in_hbm(head_t),
    )


CHUNKS = 4
CROWS = ROWS // CHUNKS
HROWS = CROWS // 2
TP = 4
WIDTH = D // TP
HALF = D // 2
QUART = HALF // 2
PAIR = 256
MESH = pl.DeviceIdType.MESH
N_COPIES = 124


def tail_kernel(
    attn_ref,
    gain_ref,
    tok_hbm,
    wo_ref,
    hw_ref,
    states_ref,
    norms_ref,
    max_ref,
    logits_ref,
    tok_v,
    own_state,
    gathered,
    last_out,
    last_in,
    far_out,
    far_l,
    far_r,
    part_r,
    part_l,
    part_own,
    near_out_r,
    near_out_l,
    near_in_l,
    near_in_r,
    mx,
    mx_in,
    tok_sem,
    send_sem,
    recv_sem,
):
    req = lax.axis_index("req")
    y = lax.axis_index("tp")
    core = lax.rem(req, 2)
    x = lax.rem(req // 2, 4)
    z = req // 8
    right, left, opp = lax.rem(y + 1, TP), lax.rem(y + 3, TP), lax.rem(y + 2, TP)

    def at(dx=0, dz=0, dc=0, dy=0):
        xx, zz, cc = lax.rem(x + dx, 4), lax.rem(z + dz, 4), lax.rem(core + dc, 2)
        return {"req": (zz * 4 + xx) * 2 + cc, "tp": lax.rem(y + dy, TP)}

    plane = [{"dx": i, "dz": j} for i in range(4) for j in range(4) if i or j]
    column = [{"dy": i, "dc": j} for i in range(4) for j in range(2) if i or j]
    peers = [at(**move) for move in plane + column]

    def wide(d):
        return pl.ds(pl.multiple_of(d * WIDTH, WIDTH), WIDTH)

    tok_copy = pltpu.make_async_copy(tok_hbm.at[:, wide(y)], tok_v, tok_sem)
    tok_copy.start()

    barrier = pltpu.get_barrier_semaphore()
    for peer in peers:
        pl.semaphore_signal(barrier, inc=1, device_id=peer, device_id_type=MESH)

    copies = {}

    def send(name, src, dst, device):
        i = len(copies)
        copies[name] = pltpu.make_async_remote_copy(
            src_ref=src,
            dst_ref=dst,
            send_sem=send_sem.at[i],
            recv_sem=recv_sem.at[i],
            device_id=device,
            device_id_type=MESH,
        )
        copies[name].start()

    def got(name):
        copies[name].wait_recv()

    pick_row = lax.broadcasted_iota(jnp.int32, (REQ_DEV, ROWS), 0)
    pick_col = lax.broadcasted_iota(jnp.int32, (REQ_DEV, ROWS), 1)
    pick = (pick_col == pick_row * NEW + (NEW - 1)).astype(jnp.bfloat16)
    attn_last = jnp.dot(pick, attn_ref[...], preferred_element_type=jnp.float32).astype(jnp.bfloat16)

    def project(dy, out_ref):
        out_ref[...] = jnp.dot(
            attn_ref[...], wo_ref[:, wide(lax.rem(y + dy, TP))], preferred_element_type=jnp.float32
        ).astype(out_ref.dtype)

    def far_send(c):
        r = c * CROWS
        send(("far", c, 1), far_out.at[r : r + HROWS], far_l.at[c], at(dy=1))
        send(("far", c, 3), far_out.at[r + HROWS : r + CROWS], far_r.at[c], at(dy=3))

    order = ((2, 0), (1, 1), (3, 2))
    for dy, i in order:
        last_out[i] = jnp.dot(
            attn_last, wo_ref[:, wide(lax.rem(y + dy, TP))], preferred_element_type=jnp.float32
        ).astype(jnp.bfloat16)
    project(2, far_out)
    pl.semaphore_wait(barrier, len(peers))
    for dy, i in order:
        send(("last", dy), last_out.at[i], last_in.at[i], at(dy=dy))
    far_send(0)
    own_last = jnp.dot(attn_last, wo_ref[:, wide(y)], preferred_element_type=jnp.float32)
    tok_copy.wait()
    own_last = own_last + jnp.dot(pick, tok_v[...], preferred_element_type=jnp.float32)
    project(1, part_r)
    for dy, i in order:
        got(("last", dy))
        own_last = own_last + last_in[i].astype(jnp.float32)
    own_rows = pl.ds(pl.multiple_of(req * REQ_DEV, REQ_DEV), REQ_DEV)
    own_state[:, wide(y)] = own_last.astype(jnp.bfloat16)
    for dy in (1, 3, 2):
        block = own_state.at[:, wide(y)]
        send(("slice", dy), block, block, at(dy=dy))
    for c in range(1, CHUNKS):
        far_send(c)
    project(3, part_l)
    for dy in (1, 3, 2):
        got(("slice", dy))
    own = own_state[...].astype(jnp.float32)
    own_norm = jnp.sqrt(jnp.sum(own * own, axis=1, keepdims=True) * (1.0 / D) + EPS)
    gathered[own_rows, :] = (own / own_norm * gain_ref[...]).astype(jnp.bfloat16)

    def device(half, df=0, ds=0):
        return at(dx=df, dz=ds) if half == 0 else at(dx=ds, dz=df)

    def piece(half, df, ds, part=None):
        d = device(half, df, ds)["req"]
        rows = pl.ds(pl.multiple_of(d * REQ_DEV, REQ_DEV), REQ_DEV)
        start, width = half * HALF, HALF
        if part is not None:
            start, width = start + part * QUART, QUART
        return gathered.at[rows, start : start + width]

    def push(name, half, df, ds, to, part=None):
        block = piece(half, df, ds, part)
        send((name, half, df, ds, part), block, block, to)

    def spread(half, k):
        for side in (1, 3):
            block = piece(half, k, 0)
            send(("second", half, k, side), block, block, device(half, 0, side))

    def sibling(half, df, ds):
        push("sib", half, df, ds, at(dc=1))

    for half in (0, 1):
        for side in (1, 3):
            block = piece(half, 0, 0)
            send(("first", half, side), block, block, device(half, side, 0))
    for half in (0, 1):
        spread(half, 0)
    for half in (0, 1):
        sibling(half, 0, 0)

    eye_row = lax.broadcasted_iota(jnp.int32, (REQ_DEV, REQ_DEV), 0)
    eye_col = lax.broadcasted_iota(jnp.int32, (REQ_DEV, REQ_DEV), 1)
    norms_ref[...] = jnp.sum(jnp.where(eye_row == eye_col, own_norm, 0.0), axis=0, keepdims=True)

    def near_step(c):
        r = c * CROWS
        got(("far", c, 1))
        near_out_r[c, 0:HROWS] = (part_r[r : r + HROWS] + far_l[c].astype(jnp.float32)).astype(jnp.bfloat16)
        near_out_r[c, HROWS:CROWS] = part_r[r + HROWS : r + CROWS].astype(jnp.bfloat16)
        send(("near", c, 1), near_out_r.at[c], near_in_l.at[c], at(dy=1))
        got(("far", c, 3))
        near_out_l[c, 0:HROWS] = part_l[r : r + HROWS].astype(jnp.bfloat16)
        near_out_l[c, HROWS:CROWS] = (part_l[r + HROWS : r + CROWS] + far_r[c].astype(jnp.float32)).astype(jnp.bfloat16)
        send(("near", c, 3), near_out_l.at[c], near_in_r.at[c], at(dy=3))

    def relay_second(half, k):
        for side, part, ds in ((1, 0, 3), (3, 1, 1)):
            got(("second", half, k, side))
            block = piece(half, k, ds, part)
            send(("third", half, k, side), block, block, device(half, 0, side))
            sibling(half, k, ds)

    def finish_second(half, k):
        for side in (1, 3):
            got(("third", half, k, side))
        sibling(half, k, 2)

    def logits_of(pair, shifts):
        for dz in shifts:
            for dx in range(4):
                got(("sib", 0, dx, dz, None))
                got(("sib", 1, dz, dx, None))
        rows = pl.ds(pl.multiple_of(pair * PAIR, PAIR), PAIR)
        out = lax.dot_general(
            hw_ref[...], gathered[rows, :], (((1,), (1,)), ((), ())), preferred_element_type=jnp.float32
        )
        logits_ref[:, rows] = out
        mx[0, pl.ds(pair, 1), :] = jnp.max(out, axis=0, keepdims=True)

    project(0, part_own)
    for half in (0, 1):
        for side, part, df in ((1, 0, 3), (3, 1, 1)):
            got(("first", half, side))
            block = piece(half, df, 0, part)
            send(("relay", half, side), block, block, device(half, side, 0))
            spread(half, df)
            sibling(half, df, 0)
    near_step(0)
    for half in (0, 1):
        relay_second(half, 0)
    for half in (0, 1):
        for side in (1, 3):
            got(("relay", half, side))
        spread(half, 2)
        sibling(half, 2, 0)
    near_step(1)
    for k in (3, 1):
        for half in (0, 1):
            relay_second(half, k)
    near_step(2)
    for half in (0, 1):
        finish_second(half, 0)
    for half in (0, 1):
        relay_second(half, 2)
    near_step(3)
    for k in (3, 1):
        for half in (0, 1):
            finish_second(half, k)
    mine, other = z // 2, 1 - z // 2

    for half in (0, 1):
        finish_second(half, 2)
    logits_of(mine, (0, 1, 3))
    logits_of(other, (2,))

    def spread_max(stage, moves):
        for i, move in enumerate(moves):
            send(("max", stage, i), mx.at[stage], mx_in.at[stage, i], at(**move))

    def take_max(stage, moves):
        m = mx[stage]
        for i in range(len(moves)):
            got(("max", stage, i))
            m = jnp.maximum(m, mx_in[stage, i])
        return m

    spread_max(0, plane)
    mx[1] = take_max(0, plane)
    spread_max(1, column)

    for c in range(CHUNKS):
        r = slice(c * CROWS, (c + 1) * CROWS)
        got(("near", c, 1))
        got(("near", c, 3))
        total = tok_v[r].astype(jnp.float32) + part_own[r] + near_in_l[c].astype(jnp.float32)
        states_ref[r] = (total + near_in_r[c].astype(jnp.float32)).astype(jnp.bfloat16)
    max_ref[...] = take_max(1, column)
    for c in copies.values():
        c.wait_send()


def tail_call(attention, gain, tokens, w_out, head_t):
    vmem = pl.BlockSpec(memory_space=pltpu.VMEM)
    hbm = pl.BlockSpec(memory_space=pltpu.HBM)
    half = jnp.bfloat16
    return pl.pallas_call(
        tail_kernel,
        out_shape=(
            jax.ShapeDtypeStruct((ROWS, WIDTH), half),
            jax.ShapeDtypeStruct((1, REQ_DEV), jnp.float32),
            jax.ShapeDtypeStruct((2, PAIR), jnp.float32),
            jax.ShapeDtypeStruct((VLOC, 2 * PAIR), jnp.float32),
        ),
        in_specs=[vmem, vmem, hbm, vmem, vmem],
        out_specs=(vmem, vmem, vmem, vmem),
        scratch_shapes=[
            pltpu.VMEM((ROWS, WIDTH), half),
            pltpu.VMEM((REQ_DEV, D), half),
            pltpu.VMEM((2 * PAIR, D), half),
            pltpu.VMEM((3, REQ_DEV, WIDTH), half),
            pltpu.VMEM((3, REQ_DEV, WIDTH), half),
            pltpu.VMEM((ROWS, WIDTH), half),
            pltpu.VMEM((CHUNKS, HROWS, WIDTH), half),
            pltpu.VMEM((CHUNKS, HROWS, WIDTH), half),
            pltpu.VMEM((ROWS, WIDTH), jnp.float32),
            pltpu.VMEM((ROWS, WIDTH), jnp.float32),
            pltpu.VMEM((ROWS, WIDTH), jnp.float32),
            pltpu.VMEM((CHUNKS, CROWS, WIDTH), half),
            pltpu.VMEM((CHUNKS, CROWS, WIDTH), half),
            pltpu.VMEM((CHUNKS, CROWS, WIDTH), half),
            pltpu.VMEM((CHUNKS, CROWS, WIDTH), half),
            pltpu.VMEM((2, 2, PAIR), jnp.float32),
            pltpu.VMEM((2, 15, 2, PAIR), jnp.float32),
            pltpu.SemaphoreType.DMA,
            pltpu.SemaphoreType.DMA((N_COPIES,)),
            pltpu.SemaphoreType.DMA((N_COPIES,)),
        ],
        compiler_params=pltpu.CompilerParams(
            vmem_limit_bytes=28 * 1024 * 1024, collective_id=0, has_side_effects=True
        ),
        name="tail",
    )(attention, gain.reshape(1, D), in_hbm(tokens), w_out, head_t)


def local(
    tokens,
    w_query,
    query_bias,
    w_keyval,
    keyval_bias,
    w_out,
    attn_gain,
    final_norm_gain,
    head_weight,
    kv_pool,
    cache_len,
):
    new_kv, attention, w_out_v, head_v = attention_call(
        cache_len,
        tokens,
        w_query,
        w_keyval,
        query_bias,
        keyval_bias,
        attn_gain,
        kv_pool.reshape(POOL, KW),
        w_out,
        head_weight.T,
    )
    states, norms, top, logits_t = tail_call(attention, final_norm_gain, tokens, w_out_v, head_v)
    return (
        states,
        new_kv.reshape(ROWS, 1, KW),
        norms.reshape(REQ_DEV),
        top.reshape(2 * PAIR),
        logits_t.T,
    )


def solution(mesh):
    return jax.shard_map(
        local,
        mesh=mesh,
        in_specs=(
            P("req", None),
            P(None, "tp"),
            P("tp"),
            P(None, "tp"),
            P("tp"),
            P("tp", None),
            P(),
            P(),
            P(None, ("req", "tp")),
            P("req", "tp", None),
            P(),
        ),
        out_specs=(P("req", "tp"), P("req", "tp", None), P("req"), P(), P(None, ("req", "tp"))),
        check_vma=False,
    )
```

time: 98.6 us -> 76 us (0.77)
  Pallas kernels: 87.8 us -> 71.1 us
  local copies, waits for them, and re-layouts: 9.75 us -> 3.07 us
    pallas_call x1, Pallas kernels: 70.6 us -> 57.5 us  [tail_call(): pl.pallas_call(tail_kernel, out_shape=(jax.ShapeDtypeStruct((ROWS, WIDTH)...]
    unnamed x16 -> x6, local copies, waits for them, and re-layouts: 9.06 us -> 3.07 us
    pallas_call x1, Pallas kernels: 17.2 us -> 13.6 us  [attention_call(): pl.pallas_call(attn_kernel, out_shape=(jax.ShapeDtypeStruct((ROWS, KW), j...]
where the time goes in v3:
time: 76 us; the launch traced here: 74.9 us
  Pallas kernels  71.1 us (94%)
  local copies, waits for them, and re-layouts  3.07 us (4%)
    pallas_call x1, Pallas kernels, tail_call(): pl.pallas_call(tail_kernel, out_shape=(jax.ShapeDtypeStruct((ROWS, WIDTH)...  57.5 us
    pallas_call x1, Pallas kernels, attention_call(): pl.pallas_call(attn_kernel, out_shape=(jax.ShapeDtypeStruct((ROWS, KW), j...  13.6 us
    unnamed x6, local copies, waits for them, and re-layouts  3.07 us

profile of v3, /device:TPU:0, one launch (start us, length us, event | category | flops | bytes accessed | tf_op | source)
XLA Modules:
  0.0 74.9 jit_solution(14626311225757072929)
XLA Ops:
  0.6 0.0 copy-start
  0.6 13.6 %attend.1 = (bf16[384,256]{1,0:T(8,128)(2,1)}, bf16[384,640]{1,0:T(8,128)(2,1)S(1)}, bf16[640,5120]{1,0:T(8,128)(2,1)S(1)}, bf16[594,5120]{1,0:T(8,128)(2,1)S(1)}) custom-call(s32[512]{0:T(512)} %lens_hbm.1, bf16[384,5120]{1,0:T(8,128)(2,1)} %tok_hbm.3, bf16[5120,640]{1,0:T(8,128)(2,1)} %wq_hbm.1, bf16[5120,256]{1,0:T(8,128)(2,1)} %wkv_hbm.1, f32[640]{0:T(1024)} %qb_hbm.1, ...), custom_call_target="tpu_custom_call" | custom-call | tf_op jit(solution)/shard_map/attend/pallas_call | solution.py:283
  14.2 0.0 copy-done
  14.3 57.5 %tail.1 = (bf16[384,1280]{1,0:T(8,128)(2,1)S(1)}, f32[1,16]{1,0:T(1,128)S(1)}, f32[2,256]{1,0:T(2,128)S(1)}, f32[594,512]{1,0:T(8,128)S(1)}) custom-call(bf16[384,640]{1,0:T(8,128)(2,1)S(1)} %get-tuple-element.13.attn_ref, f32[1,5120]{1,0:T(1,128)S(1)} %bitcast.9, bf16[384,5120]{1,0:T(8,128)(2,1)} %tok_hbm.3, ...), custom_call_target="tpu_custom_call" | custom-call | tf_op jit(solution)/shard_map/tail/pallas_call | solution.py:604
  71.8 0.6 copy.17
  72.4 0.9 %copy.21 = bf16[384,1280]{1,0:T(8,128)(2,1)} copy(bf16[384,1280]{1,0:T(8,128)(2,1)S(1)} %get-tuple-element.26) | data formatting | bytes 1966080
  73.3 0.5 copy.22
  73.9 1.0 %copy.23 = f32[512,594]{0,1:T(8,128)} copy(f32[512,594]{0,1:T(8,128)S(1)} %bitcast.8) | data formatting | bytes 2433024
Async XLA Ops:
  0.6 13.6 %copy-start = (f32[5120]{0:T(1024)S(1)}, f32[5120]{0:T(1024)}, u32[]{:S(2)}) copy-start(f32[5120]{0:T(1024)} %param.19) | copy-start | bytes 61444

commit v4 on v3

--- a/solution.py
+++ b/solution.py
@@ -150,9 +150,6 @@
         ss[...] += part
         xg = (x * gain_v[c].reshape(1, KC)).astype(jnp.bfloat16)
         acc[...] += jnp.dot(xg, w_v[c, :], preferred_element_type=jnp.float32)
-    for c in tails:
-        c.start()
-
     for c in smalls[2:]:
         c.wait()
     rstd = 1.0 / jnp.sqrt(jnp.sum(ss[...], axis=1, keepdims=True) * (1.0 / D) + EPS)
@@ -237,7 +234,10 @@
             store_heads(r, outs[i] / ls[i])
         return jnp.maximum(waited, need)
 
-    waited = lax.fori_loop(0, REQ_DEV // BATCH, batch, jnp.int32(0))
+    waited = lax.fori_loop(0, REQ_DEV // BATCH - 1, batch, jnp.int32(0))
+    for c in tails:
+        c.start()
+    waited = batch(REQ_DEV // BATCH - 1, waited)
     lax.fori_loop(waited, NPC, wait_one, 0)
 
     def longs(j, carry):
@@ -316,7 +316,7 @@
             pltpu.SemaphoreType.DMA((5,)),
             pltpu.SemaphoreType.DMA((2,)),
         ],
-        compiler_params=pltpu.CompilerParams(vmem_limit_bytes=36 * 1024 * 1024),
+        compiler_params=pltpu.CompilerParams(vmem_limit_bytes=38 * 1024 * 1024),
         name="attend",
     )(
         in_hbm(cache_len),
@@ -536,20 +536,25 @@
         mx[0, pl.ds(pair, 1), :] = jnp.max(out, axis=0, keepdims=True)
 
     project(0, part_own)
-    for half in (0, 1):
-        for side, part, df in ((1, 0, 3), (3, 1, 1)):
+    for side, part, df in ((1, 0, 3), (3, 1, 1)):
+        for half in (0, 1):
             got(("first", half, side))
             block = piece(half, df, 0, part)
             send(("relay", half, side), block, block, device(half, side, 0))
-            spread(half, df)
-            sibling(half, df, 0)
+    for half in (0, 1):
+        spread(half, 3)
+        spread(half, 1)
+    for half in (0, 1):
+        sibling(half, 3, 0)
+        sibling(half, 1, 0)
     near_step(0)
-    for half in (0, 1):
-        relay_second(half, 0)
     for half in (0, 1):
         for side in (1, 3):
             got(("relay", half, side))
         spread(half, 2)
+    for half in (0, 1):
+        relay_second(half, 0)
+    for half in (0, 1):
         sibling(half, 2, 0)
     near_step(1)
     for k in (3, 1):
@@ -592,7 +597,10 @@
         got(("near", c, 3))
         total = tok_v[r].astype(jnp.float32) + part_own[r] + near_in_l[c].astype(jnp.float32)
         states_ref[r] = (total + near_in_r[c].astype(jnp.float32)).astype(jnp.bfloat16)
-    max_ref[...] = take_max(1, column)
+    top = take_max(1, column)
+    for i in range(4):
+        h = HD * (i % 2)
+        max_ref[i : i + 1, :] = top[i // 2 : i // 2 + 1, h : h + HD]
     for c in copies.values():
         c.wait_send()
 
@@ -606,7 +614,7 @@
         out_shape=(
             jax.ShapeDtypeStruct((ROWS, WIDTH), half),
             jax.ShapeDtypeStruct((1, REQ_DEV), jnp.float32),
-            jax.ShapeDtypeStruct((2, PAIR), jnp.float32),
+            jax.ShapeDtypeStruct((4, HD), jnp.float32),
             jax.ShapeDtypeStruct((VLOC, 2 * PAIR), jnp.float32),
         ),
         in_specs=[vmem, vmem, hbm, vmem, vmem],
@@ -640,6 +648,28 @@
     )(attention, gain.reshape(1, D), in_hbm(tokens), w_out, head_t)
 
 
+def out_kernel(*refs):
+    n = len(refs) // 2
+    sems = refs[-1]
+    moves = [pltpu.make_async_copy(refs[i], refs[n + i], sems.at[i]) for i in range(n)]
+    for m in moves:
+        m.start()
+    for m in moves:
+        m.wait()
+
+
+def out_call(*arrays):
+    return pl.pallas_call(
+        out_kernel,
+        out_shape=tuple(jax.ShapeDtypeStruct(a.shape, a.dtype) for a in arrays),
+        in_specs=[pl.BlockSpec(memory_space=pltpu.VMEM)] * len(arrays),
+        out_specs=tuple(pl.BlockSpec(memory_space=pltpu.HBM) for _ in arrays),
+        scratch_shapes=[pltpu.SemaphoreType.DMA((len(arrays),))],
+        compiler_params=pltpu.CompilerParams(vmem_limit_bytes=4 * 1024 * 1024),
+        name="write",
+    )(*arrays)
+
+
 def local(
     tokens,
     w_query,
@@ -665,7 +695,7 @@
         w_out,
         head_weight.T,
     )
-    states, norms, top, logits_t = tail_call(attention, final_norm_gain, tokens, w_out_v, head_v)
+    states, norms, top, logits_t = out_call(*tail_call(attention, final_norm_gain, tokens, w_out_v, head_v))
     return (
         states,
         new_kv.reshape(ROWS, 1, KW),

time: 76 us -> 71.9 us (0.946)
  local copies, waits for them, and re-layouts: 3.07 us -> 0.01 us
  Pallas kernels: 71.1 us -> 69.9 us
    pallas_call x1, Pallas kernels: 57.5 us -> 53.7 us  [tail_call(): pl.pallas_call(tail_kernel, out_shape=(jax.ShapeDtypeStruct((ROWS, WIDTH)...]
    unnamed x6 -> x2, local copies, waits for them, and re-layouts: 3.07 us -> 0.01 us
    pallas_call x0 -> x1, Pallas kernels: none -> 1.4 us  [out_call(): pl.pallas_call(out_kernel, out_shape=tuple((jax.ShapeDtypeStruct(a.shape,...]
    pallas_call x1, Pallas kernels: 13.6 us -> 14.8 us  [attention_call(): pl.pallas_call(attn_kernel, out_shape=(jax.ShapeDtypeStruct((ROWS, KW), j...]
where the time goes in v4:
time: 71.9 us; the launch traced here: 70.8 us
  Pallas kernels  69.9 us (97%)
  between operations  0.83 us (1%)
    pallas_call x1, Pallas kernels, tail_call(): pl.pallas_call(tail_kernel, out_shape=(jax.ShapeDtypeStruct((ROWS, WIDTH)...  53.7 us
    pallas_call x1, Pallas kernels, attention_call(): pl.pallas_call(attn_kernel, out_shape=(jax.ShapeDtypeStruct((ROWS, KW), j...  14.8 us

profile of v4, /device:TPU:0, one launch (start us, length us, event | category | flops | bytes accessed | tf_op | source)
XLA Modules:
  0.0 70.8 jit_solution(16581825514420168814)
XLA Ops:
  0.6 0.0 copy-start
  0.6 14.8 %attend.1 = (bf16[384,256]{1,0:T(8,128)(2,1)}, bf16[384,640]{1,0:T(8,128)(2,1)S(1)}, bf16[640,5120]{1,0:T(8,128)(2,1)S(1)}, bf16[594,5120]{1,0:T(8,128)(2,1)S(1)}) custom-call(s32[512]{0:T(512)} %lens_hbm.1, bf16[384,5120]{1,0:T(8,128)(2,1)} %tok_hbm.3, bf16[5120,640]{1,0:T(8,128)(2,1)} %wq_hbm.1, bf16[5120,256]{1,0:T(8,128)(2,1)} %wkv_hbm.1, f32[640]{0:T(1024)} %qb_hbm.1, ...), custom_call_target="tpu_custom_call" | custom-call | tf_op jit(solution)/shard_map/attend/pallas_call | solution.py:283
  15.5 0.0 copy-done
  15.5 53.7 %tail.1 = (bf16[384,1280]{1,0:T(8,128)(2,1)S(1)}, f32[1,16]{1,0:T(1,128)S(1)}, f32[4,128]{1,0:T(4,128)S(1)}, f32[594,512]{1,0:T(8,128)S(1)}) custom-call(bf16[384,640]{1,0:T(8,128)(2,1)S(1)} %get-tuple-element.17.attn_ref, f32[1,5120]{1,0:T(1,128)S(1)} %bitcast.7, bf16[384,5120]{1,0:T(8,128)(2,1)} %tok_hbm.3, ...), custom_call_target="tpu_custom_call" | custom-call | tf_op jit(solution)/shard_map/tail/pallas_call | solution.py:612
  69.2 1.4 %write.1 = (bf16[384,1280]{1,0:T(8,128)(2,1)}, f32[1,16]{1,0:T(1,128)}, f32[4,128]{1,0:T(4,128)}, f32[594,512]{1,0:T(8,128)}) custom-call(bf16[384,1280]{1,0:T(8,128)(2,1)S(1)} %get-tuple-element.20.refs_0_, f32[1,16]{1,0:T(1,128)S(1)} %get-tuple-element.21.refs_1_, f32[4,128]{1,0:T(4,128)S(1)} %get-tuple-element.22.refs_2_, ...), custom_call_target="tpu_custom_call" | custom-call | tf_op jit(solution)/shard_map/write/pallas_call | solution.py:662
Async XLA Ops:
  0.6 14.9 %copy-start = (f32[5120]{0:T(1024)S(1)}, f32[5120]{0:T(1024)}, u32[]{:S(2)}) copy-start(f32[5120]{0:T(1024)} %param.19) | copy-start | bytes 61444

commit v5 on v4

--- a/solution.py
+++ b/solution.py
@@ -29,7 +29,8 @@
 PC = 2048
 NPC = POOL // PC
 QR = 128
-PER_STEP = 4
+AHEAD = 3
+PER_STEP = 5
 BATCH = 4
 WIDE = (LONG - SHORT) // 2
 VLOC = 594
@@ -113,10 +114,13 @@
     ]
     smalls[0].start()
     smalls[1].start()
-    for k in range(NKC):
+    def feed(k):
         tok_copy(k).start()
         wq_copy(k).start()
         wkv_copy(k).start()
+
+    for k in range(AHEAD):
+        feed(k)
     for c in smalls[2:]:
         c.start()
     ss[...] = jnp.zeros_like(ss)
@@ -138,8 +142,11 @@
         tok_copy(k).wait()
         wq_copy(k).wait()
         wkv_copy(k).wait()
-        if k >= 1:
-            for i in range(PER_STEP * (k - 1), min(PER_STEP * k, NPC)):
+        if k + AHEAD < NKC:
+            feed(k + AHEAD)
+        else:
+            first = k + AHEAD - NKC
+            for i in range(PER_STEP * first, min(PER_STEP * (first + 1), NPC)):
                 pool_copy(i).start()
         c = slice(k * KC, (k + 1) * KC)
         x = tok_v[:, c].astype(jnp.float32)

time: 71.9 us -> 71.5 us (level)
  no operation moved by 1% of the time
where the time goes in v5:
time: 71.5 us; the launch traced here: 70.1 us
  Pallas kernels  69.3 us (97%)
  between operations  0.83 us (1%)
    pallas_call x1, Pallas kernels, tail_call(): pl.pallas_call(tail_kernel, out_shape=(jax.ShapeDtypeStruct((ROWS, WIDTH)...  53.6 us
    pallas_call x1, Pallas kernels, attention_call(): pl.pallas_call(attn_kernel, out_shape=(jax.ShapeDtypeStruct((ROWS, KW), j...  14.3 us

profile of v5, /device:TPU:0, one launch (start us, length us, event | category | flops | bytes accessed | tf_op | source)
XLA Modules:
  0.0 70.1 jit_solution(6773375763261931307)
XLA Ops:
  0.6 0.0 copy-start
  0.6 14.3 %attend.1 = (bf16[384,256]{1,0:T(8,128)(2,1)}, bf16[384,640]{1,0:T(8,128)(2,1)S(1)}, bf16[640,5120]{1,0:T(8,128)(2,1)S(1)}, bf16[594,5120]{1,0:T(8,128)(2,1)S(1)}) custom-call(s32[512]{0:T(512)} %lens_hbm.1, bf16[384,5120]{1,0:T(8,128)(2,1)} %tok_hbm.3, bf16[5120,640]{1,0:T(8,128)(2,1)} %wq_hbm.1, bf16[5120,256]{1,0:T(8,128)(2,1)} %wkv_hbm.1, f32[640]{0:T(1024)} %qb_hbm.1, ...), custom_call_target="tpu_custom_call" | custom-call | tf_op jit(solution)/shard_map/attend/pallas_call | solution.py:290
  14.9 0.0 copy-done
  14.9 53.6 %tail.1 = (bf16[384,1280]{1,0:T(8,128)(2,1)S(1)}, f32[1,16]{1,0:T(1,128)S(1)}, f32[4,128]{1,0:T(4,128)S(1)}, f32[594,512]{1,0:T(8,128)S(1)}) custom-call(bf16[384,640]{1,0:T(8,128)(2,1)S(1)} %get-tuple-element.17.attn_ref, f32[1,5120]{1,0:T(1,128)S(1)} %bitcast.7, bf16[384,5120]{1,0:T(8,128)(2,1)} %tok_hbm.3, ...), custom_call_target="tpu_custom_call" | custom-call | tf_op jit(solution)/shard_map/tail/pallas_call | solution.py:619
  68.5 1.4 %write.1 = (bf16[384,1280]{1,0:T(8,128)(2,1)}, f32[1,16]{1,0:T(1,128)}, f32[4,128]{1,0:T(4,128)}, f32[594,512]{1,0:T(8,128)}) custom-call(bf16[384,1280]{1,0:T(8,128)(2,1)S(1)} %get-tuple-element.20.refs_0_, f32[1,16]{1,0:T(1,128)S(1)} %get-tuple-element.21.refs_1_, f32[4,128]{1,0:T(4,128)S(1)} %get-tuple-element.22.refs_2_, ...), custom_call_target="tpu_custom_call" | custom-call | tf_op jit(solution)/shard_map/write/pallas_call | solution.py:669
Async XLA Ops:
  0.6 14.3 %copy-start = (f32[5120]{0:T(1024)S(1)}, f32[5120]{0:T(1024)}, u32[]{:S(2)}) copy-start(f32[5120]{0:T(1024)} %param.19) | copy-start | bytes 61444
